TPU v7x, 512 devices: a whole 4x8x8 slice. The times are simulated.
512 devices in a mesh: tile: 128 (over z, y, core), lev: 4 (over x).
Axes of the slice: x: 4, y: 8, z: 8, core: 2. Of those that a mesh axis runs over, the one named last changes fastest.
Arguments:
- adj_out: bfloat16 [512, 8, 3, 128, 128], P('tile', 'lev'), may hold values from -6 to 6
- lat_weights: bfloat16 [8, 128, 128], replicated, may hold values from -0.5 to 0.5
- lon_weights: bfloat16 [8, 128, 128], replicated, may hold values from -0.5 to 0.5
- counts: int32 [512], P('tile'), may hold values from 2 to 12, as said below
- departures: int32 [512, 12], P('tile'), may hold values from 0 to 511, as said below
- blocks: int32 [512, 12, 2], P('tile'), may hold values from 0 to 7
- upper_coef: bfloat16 [512, 8, 128, 128], P('tile', 'lev'), may hold values from 0.19921875 to 1
- lower_coef: bfloat16 [512, 8, 128, 128], P('tile', 'lev'), may hold values from 0.19921875 to 1
Outputs:
- adj_in: bfloat16 [512, 8, 3, 128, 128], P('tile', 'lev')
Inputs may be any that keep to these rules, and one draw needn't show every extreme that they name: `counts`: every tile has 2 to 12 live slots; some tiles have exactly 12. The 4 tiles of one index of tile hold at most 27 live slots together, and some index of tile holds exactly 27. `departures`: every slot's source tile, live or not, belongs to an index of tile at most 2 places away from the index that holds the slot's tile, counted around the tile axis with wrap-around.
All inputs are finite; a program needn't handle non-finite values.
Results may differ from a plain program's by a relative error of at most 0.0062.
Values may be sent and summed in bfloat16 or wider, within the bound.
No kernel may reach another device: no remote copies, remote signals or barrier semaphores. Data moves between devices by JAX's collectives and lax.ppermute only.
A program may use at most 128 MiB of HBM per device.

v0:
```python
import jax
import jax.numpy as jnp
from jax import lax
from jax.sharding import PartitionSpec as P

REACH = 2


def from_behind(value, axis, steps):
    count = lax.axis_size(axis)
    pairs = [(source, (source + steps) % count) for source in range(count)]
    return lax.ppermute(value, axis, pairs)


def passed_along(x, axis, by):
    length = lax.axis_size(axis)
    pairs = [(i, i + by) for i in range(length) if 0 <= i + by < length]
    return lax.ppermute(x, axis, pairs)


def slot_terms(lat_applied, lon_sel, pick_table):
    slot_part = jnp.einsum(
        "klfbc,kcd->klfbd", lat_applied, lon_sel, preferred_element_type=jnp.float32
    ).astype(jnp.bfloat16)
    return jnp.einsum("kw,klfbd->wlfbd", pick_table, slot_part, preferred_element_type=jnp.float32)


def per_device(
    adj_out, lat_weights, lon_weights, counts, departures, blocks, upper_coef, lower_coef
):
    tile_devices = lax.axis_size("tile")
    own_index = lax.axis_index("tile")
    tile_count, slot_count = departures.shape
    window = (2 * REACH + 1) * tile_count
    all_tiles = tile_devices * tile_count
    base_tile = (own_index - REACH) % tile_devices * tile_count
    local_rows = (departures - base_tile) % all_tiles
    live_mask = jnp.arange(slot_count, dtype=jnp.int32)[None, :] < counts[:, None]
    columns = jnp.arange(window, dtype=jnp.int32)
    pick_all = ((local_rows[:, :, None] == columns[None, None, :]) & live_mask[:, :, None]).astype(
        jnp.bfloat16
    )
    bundle = jnp.zeros((window,) + adj_out.shape[1:], jnp.float32)
    for tile_pos in range(tile_count):
        lat_sel = jnp.take(lat_weights, blocks[tile_pos, :, 0], axis=0)
        lon_sel = jnp.take(lon_weights, blocks[tile_pos, :, 1], axis=0)
        lat_applied = jnp.einsum(
            "kab,lfac->klfbc", lat_sel, adj_out[tile_pos], preferred_element_type=jnp.float32
        ).astype(jnp.bfloat16)
        bundle = bundle + slot_terms(lat_applied, lon_sel, pick_all[tile_pos])
    sending = bundle.astype(jnp.bfloat16).reshape((2 * REACH + 1, tile_count) + adj_out.shape[1:])
    interp = sending[REACH].astype(jnp.float32)
    for offset in range(-REACH, REACH + 1):
        if offset != 0:
            arrived = from_behind(sending[offset + REACH], "tile", offset)
            interp = interp + arrived.astype(jnp.float32)
    upper_rate = upper_coef.astype(jnp.float32)[:, :, None]
    lower_rate = lower_coef.astype(jnp.float32)[:, :, None]
    upflow = upper_rate * interp
    downflow = lower_rate * interp
    lower_rim = passed_along(upflow[:, -1].astype(jnp.bfloat16), "lev", 1).astype(jnp.float32)
    upper_rim = passed_along(downflow[:, 0].astype(jnp.bfloat16), "lev", -1).astype(jnp.float32)
    from_lower = jnp.concatenate([lower_rim[:, None], upflow[:, :-1]], axis=1)
    from_upper = jnp.concatenate([downflow[:, 1:], upper_rim[:, None]], axis=1)
    return ((1.0 + upper_rate + lower_rate) * interp - from_lower - from_upper).astype(jnp.bfloat16)


def solution(mesh):
    placed = (
        P("tile", "lev", None, None, None),
        P(),
        P(),
        P("tile"),
        P("tile", None),
        P("tile", None, None),
        P("tile", "lev", None, None),
        P("tile", "lev", None, None),
    )
    return jax.shard_map(
        per_device,
        mesh=mesh,
        in_specs=placed,
        out_specs=P("tile", "lev", None, None, None),
        check_vma=False,
    )
```

profile of v0, /device:TPU:1, one launch (start us, length us, event | category | flops | bytes accessed | tf_op | source)
XLA Modules:
  0.0 113.8 jit_solution(17535507239967063253)
XLA Ops:
  0.0 0.8 compare_and_fusion.1
  0.9 0.7 iota_compare_fusion.1
  1.6 0.6 gather_fusion.4
  2.3 1.3 %gather_fusion.2 = bf16[12,128,128]{2,1,0:T(8,128)(2,1)} fusion(bf16[8,128,128]{2,1,0:T(8,128)(2,1)S(1)} %copy-done, s32[1024]{0:T(1024)S(1)} %get-tuple-element.47), kind=kCustom, calls=%fused_computation.2.clone | custom fusion | bytes 786480 | tf_op jit(solution)/shard_map/jit(_take)/gather | solution.py:45
  3.6 2.3 %gather_fusion.5 = bf16[12,128,128]{2,1,0:T(8,128)(2,1)} fusion(bf16[8,128,128]{2,1,0:T(8,128)(2,1)} %param.12, s32[1024]{0:T(1024)S(1)} %get-tuple-element.44), kind=kCustom, calls=%fused_computation.5.clone | custom fusion | bytes 786480 | tf_op jit(solution)/shard_map/jit(_take)/gather | solution.py:46
  5.9 1.4 %gather_fusion.3 = bf16[12,128,128]{2,1,0:T(8,128)(2,1)} fusion(bf16[8,128,128]{2,1,0:T(8,128)(2,1)S(1)} %copy-done.1, s32[1024]{0:T(1024)S(1)} %get-tuple-element.46), kind=kCustom, calls=%fused_computation.3.clone | custom fusion | bytes 786480 | tf_op jit(solution)/shard_map/jit(_take)/gather | solution.py:46
  7.4 2.7 %fusion.33 = bf16[12,2,3,128,128]{4,3,2,1,0:T(8,128)(2,1)S(1)} fusion(bf16[12,128,128]{2,1,0:T(8,128)(2,1)} %gather_fusion.5, bf16[12,128,128]{2,1,0:T(8,128)(2,1)S(1)} %gather_fusion.4, pred[12]{0:T(512)(128)(4,1)S(1)} %get-tuple-element.28, pred[12]{0:T(512)(128)(4,1)S(1)} %get-tuple-element.30, bf16[4,2,3,128,128]{4,3,2,1,0:T(8,128)(2,1)} %param.10), kind=kOutput, calls=%fused_computation.34 | convolution fusion | flops 606732288 | bytes 3342360 | tf_op jit(solution)/shard_map/klfbc,kcd->klfbd/dot_general | solution.py:22
  10.0 4.8 %fusion.1 = f32[20,2,3,128,128]{4,0,3,2,1:T(8,128)} fusion(bf16[12,2,3,128,128]{4,3,2,1,0:T(8,128)(2,1)S(1)} %fusion.33, pred[4,12,20]{2,1,0:T(8,128)(4,1)S(1)} %fusion.103), kind=kOutput, calls=%fused_computation.10 | convolution fusion | flops 47185920 | bytes 10225664 | tf_op jit(solution)/shard_map/kw,klfbd->wlfbd/dot_general | solution.py:25
  14.8 2.7 %fusion.30 = bf16[12,2,3,128,128]{4,3,2,1,0:T(8,128)(2,1)S(1)} fusion(bf16[12,128,128]{2,1,0:T(8,128)(2,1)} %gather_fusion.3, bf16[12,128,128]{2,1,0:T(8,128)(2,1)S(1)} %copy-done.2, pred[12]{0:T(512)(128)(4,1)S(1)} %get-tuple-element.32, pred[12]{0:T(512)(128)(4,1)S(1)} %get-tuple-element.34, bf16[4,2,3,128,128]{4,3,2,1,0:T(8,128)(2,1)} %param.10), kind=kOutput, calls=%fused_computation.33 | convolution fusion | flops 606732288 | bytes 3342360 | tf_op jit(solution)/shard_map/klfbc,kcd->klfbd/dot_general | solution.py:22
  17.5 4.8 %fusion.3 = f32[20,2,3,128,128]{4,0,3,2,1:T(8,128)} fusion(bf16[12,2,3,128,128]{4,3,2,1,0:T(8,128)(2,1)S(1)} %fusion.30, pred[4,12,20]{2,1,0:T(8,128)(4,1)S(1)} %fusion.103), kind=kOutput, calls=%fused_computation.12 | convolution fusion | flops 47185920 | bytes 10225664 | tf_op jit(solution)/shard_map/kw,klfbd->wlfbd/dot_general | solution.py:25
  22.4 0.6 gather_fusion
  23.0 1.4 %gather_fusion.1 = bf16[12,128,128]{2,1,0:T(8,128)(2,1)} fusion(bf16[8,128,128]{2,1,0:T(8,128)(2,1)S(1)} %copy-done.1, s32[1024]{0:T(1024)S(1)} %get-tuple-element.48), kind=kCustom, calls=%fused_computation.1.clone | custom fusion | bytes 786480 | tf_op jit(solution)/shard_map/jit(_take)/gather | solution.py:46
  24.3 2.6 %fusion.27 = bf16[12,2,3,128,128]{4,3,2,1,0:T(8,128)(2,1)S(1)} fusion(bf16[12,128,128]{2,1,0:T(8,128)(2,1)} %gather_fusion.1, bf16[12,128,128]{2,1,0:T(8,128)(2,1)S(1)} %gather_fusion, pred[12]{0:T(512)(128)(4,1)S(1)} %get-tuple-element.36, pred[12]{0:T(512)(128)(4,1)S(1)} %get-tuple-element.38, bf16[4,2,3,128,128]{4,3,2,1,0:T(8,128)(2,1)} %param.10), kind=kOutput, calls=%fused_computation.32 | convolution fusion | flops 606732288 | bytes 3342360 | tf_op jit(solution)/shard_map/klfbc,kcd->klfbd/dot_general | solution.py:22
  27.0 4.8 %fusion.5 = f32[20,2,3,128,128]{4,0,3,2,1:T(8,128)} fusion(bf16[12,2,3,128,128]{4,3,2,1,0:T(8,128)(2,1)S(1)} %fusion.27, pred[4,12,20]{2,1,0:T(8,128)(4,1)S(1)} %fusion.103), kind=kOutput, calls=%fused_computation.14 | convolution fusion | flops 47185920 | bytes 10225664 | tf_op jit(solution)/shard_map/kw,klfbd->wlfbd/dot_general | solution.py:25
  32.4 0.6 gather_fusion.7
  33.1 2.5 %fusion.36 = bf16[12,2,3,128,128]{4,3,2,1,0:T(8,128)(2,1)S(1)} fusion(bf16[12,128,128]{2,1,0:T(8,128)(2,1)S(1)} %gather_fusion.7, bf16[12,128,128]{2,1,0:T(8,128)(2,1)S(1)} %gather_fusion.6, pred[12]{0:T(512)(128)(4,1)S(1)} %get-tuple-element.40, pred[12]{0:T(512)(128)(4,1)S(1)} %get-tuple-element.8, bf16[4,2,3,128,128]{4,3,2,1,0:T(8,128)(2,1)} %param.10), kind=kOutput, calls=%fused_computation.35 | convolution fusion | flops 606732288 | bytes 3342360 | tf_op jit(solution)/shard_map/klfbc,kcd->klfbd/dot_general | solution.py:22
  35.5 10.9 %add_convert_fusion = bf16[20,2,3,128,128]{4,0,3,2,1:T(8,128)(2,1)S(1)} fusion(f32[20,2,3,128,128]{4,0,3,2,1:T(8,128)} %fusion.1, f32[20,2,3,128,128]{4,0,3,2,1:T(8,128)} %fusion.5, f32[20,2,3,128,128]{4,0,3,2,1:T(8,128)} %fusion.3, bf16[12,2,3,128,128]{4,3,2,1,0:T(8,128)(2,1)S(1)} %fusion.36, pred[4,12,20]{2,1,0:T(8,128)(4,1)S(1)} %fusion.103), kind=kOutput, calls=%fused_computation.8 | convolution fusion | flops 55050240 | bytes 29886464 | tf_op jit(solution)/shard_map/kw,klfbd->wlfbd/dot_general | solution.py:25
  46.5 1.6 %fusion.113 = (bf16[4,2,3,128,128]{4,0,3,2,1:T(4,128)(2,1)S(1)}, bf16[4,2,3,128,128]{4,0,3,2,1:T(4,128)(2,1)S(1)}, bf16[4,2,3,128,128]{4,0,3,2,1:T(4,128)(2,1)S(1)}, bf16[4,2,3,128,128]{4,0,3,2,1:T(4,128)(2,1)S(1)}) fusion(bf16[20,2,3,128,128]{4,0,3,2,1:T(8,128)(2,1)S(1)} %add_convert_fusion), kind=kLoop, calls=%fused_computation.124 | loop fusion | bytes 6291456 | tf_op jit(solution)/shard_map/slice | solution.py:55
  48.1 14.4 %collective-permute-start = (bf16[4,2,3,128,128]{4,0,3,2,1:T(4,128)(2,1)S(1)}, bf16[4,2,3,128,128]{4,0,3,2,1:T(4,128)(2,1)S(1)}, u32[]{:S(2)}, u32[]{:S(2)}) collective-permute-start(bf16[4,2,3,128,128]{4,0,3,2,1:T(4,128)(2,1)S(1)} %get-tuple-element.24), channel_id=1, source_target_pairs={{0,504},{4,508},{8,0},{12,4},{16,8},{20,12},{24,16},{28,20},{32,24... | collective-permute-start | bytes 2359304 | tf_op jit(solution)/shard_map/ppermute | solution.py:12
  62.5 2.9 %collective-permute-start.1 = (bf16[4,2,3,128,128]{4,0,3,2,1:T(4,128)(2,1)S(1)}, bf16[4,2,3,128,128]{4,0,3,2,1:T(4,128)(2,1)S(1)}, u32[]{:S(2)}, u32[]{:S(2)}) collective-permute-start(bf16[4,2,3,128,128]{4,0,3,2,1:T(4,128)(2,1)S(1)} %get-tuple-element.27), channel_id=1, source_target_pairs={{0,508},{4,0},{8,4},{12,8},{16,12},{20,16},{24,20},{28,24},{32,28}... | collective-permute-start | bytes 2359304 | tf_op jit(solution)/shard_map/ppermute | solution.py:12
  65.4 2.7 %collective-permute-start.2 = (bf16[4,2,3,128,128]{4,0,3,2,1:T(4,128)(2,1)S(1)}, bf16[4,2,3,128,128]{4,0,3,2,1:T(4,128)(2,1)S(1)}, u32[]{:S(2)}, u32[]{:S(2)}) collective-permute-start(bf16[4,2,3,128,128]{4,0,3,2,1:T(4,128)(2,1)S(1)} %get-tuple-element.26), channel_id=1, source_target_pairs={{0,4},{4,8},{8,12},{12,16},{16,20},{20,24},{24,28},{28,32},{32,36}... | collective-permute-start | bytes 2359304 | tf_op jit(solution)/shard_map/ppermute | solution.py:12
  68.1 2.1 %collective-permute-start.3 = (bf16[4,2,3,128,128]{4,0,3,2,1:T(4,128)(2,1)S(1)}, bf16[4,2,3,128,128]{4,0,3,2,1:T(4,128)(2,1)S(1)}, u32[]{:S(2)}, u32[]{:S(2)}) collective-permute-start(bf16[4,2,3,128,128]{4,0,3,2,1:T(4,128)(2,1)S(1)} %get-tuple-element.25), channel_id=1, source_target_pairs={{0,8},{4,12},{8,16},{12,20},{16,24},{20,28},{24,32},{28,36},{32,40... | collective-permute-start | bytes 2359304 | tf_op jit(solution)/shard_map/ppermute | solution.py:12
  70.7 8.1 %collective-permute-done = bf16[4,2,3,128,128]{4,0,3,2,1:T(4,128)(2,1)S(1)} collective-permute-done((bf16[4,2,3,128,128]{4,0,3,2,1:T(4,128)(2,1)S(1)}, bf16[4,2,3,128,128]{4,0,3,2,1:T(4,128)(2,1)S(1)}, u32[]{:S(2)}, u32[]{:S(2)}) %collective-permute-start) | collective-permute-done | bytes 786464 | tf_op jit(solution)/shard_map/ppermute | solution.py:12
  78.7 4.1 %collective-permute-done.2 = bf16[4,2,3,128,128]{4,0,3,2,1:T(4,128)(2,1)S(1)} collective-permute-done((bf16[4,2,3,128,128]{4,0,3,2,1:T(4,128)(2,1)S(1)}, bf16[4,2,3,128,128]{4,0,3,2,1:T(4,128)(2,1)S(1)}, u32[]{:S(2)}, u32[]{:S(2)}) %collective-permute-start.2) | collective-permute-done | bytes 786464 | tf_op jit(solution)/shard_map/ppermute | solution.py:12
  82.9 15.8 %collective-permute-done.3 = bf16[4,2,3,128,128]{4,0,3,2,1:T(4,128)(2,1)S(1)} collective-permute-done((bf16[4,2,3,128,128]{4,0,3,2,1:T(4,128)(2,1)S(1)}, bf16[4,2,3,128,128]{4,0,3,2,1:T(4,128)(2,1)S(1)}, u32[]{:S(2)}, u32[]{:S(2)}) %collective-permute-start.3) | collective-permute-done | bytes 786464 | tf_op jit(solution)/shard_map/ppermute | solution.py:12
  98.7 1.1 broadcast_multiply_fusion
  100.1 3.1 %collective-permute-start.4 = (bf16[4,3,128,128]{3,0,2,1:T(4,128)(2,1)S(1)}, bf16[4,3,128,128]{3,0,2,1:T(4,128)(2,1)S(1)}, u32[]{:S(2)}, u32[]{:S(2)}) collective-permute-start(bf16[4,3,128,128]{3,0,2,1:T(4,128)(2,1)S(1)} %fusion.41), channel_id=1, source_target_pairs={{0,1},{1,2},{2,3},{4,5},{5,6},{6,7},{8,9},{9,10},{10,11},{12,13},{... | collective-permute-start | bytes 1179656 | tf_op jit(solution)/shard_map/ppermute | solution.py:18
  103.4 1.3 %collective-permute-start.5 = (bf16[4,3,128,128]{3,0,2,1:T(4,128)(2,1)S(1)}, bf16[4,3,128,128]{3,0,2,1:T(4,128)(2,1)S(1)}, u32[]{:S(2)}, u32[]{:S(2)}) collective-permute-start(bf16[4,3,128,128]{3,0,2,1:T(4,128)(2,1)S(1)} %fusion.42), channel_id=1, source_target_pairs={{1,0},{2,1},{3,2},{5,4},{6,5},{7,6},{9,8},{10,9},{11,10},{13,12},{... | collective-permute-start | bytes 1179656 | tf_op jit(solution)/shard_map/ppermute | solution.py:18
  105.3 2.7 %collective-permute-done.4 = bf16[4,3,128,128]{3,0,2,1:T(4,128)(2,1)S(1)} collective-permute-done((bf16[4,3,128,128]{3,0,2,1:T(4,128)(2,1)S(1)}, bf16[4,3,128,128]{3,0,2,1:T(4,128)(2,1)S(1)}, u32[]{:S(2)}, u32[]{:S(2)}) %collective-permute-start.4) | collective-permute-done | bytes 393248 | tf_op jit(solution)/shard_map/ppermute | solution.py:18
  108.0 3.9 %collective-permute-done.5 = bf16[4,3,128,128]{3,0,2,1:T(4,128)(2,1)S(1)} collective-permute-done((bf16[4,3,128,128]{3,0,2,1:T(4,128)(2,1)S(1)}, bf16[4,3,128,128]{3,0,2,1:T(4,128)(2,1)S(1)}, u32[]{:S(2)}, u32[]{:S(2)}) %collective-permute-start.5) | collective-permute-done | bytes 393248 | tf_op jit(solution)/shard_map/ppermute | solution.py:18
  112.0 0.8 fusion.40
  112.8 1.1 copy.28
  (31 shorter events, 2.2 us)
Async XLA Ops:
  0.0 1.6 %copy-start = (bf16[8,128,128]{2,1,0:T(8,128)(2,1)S(1)}, bf16[8,128,128]{2,1,0:T(8,128)(2,1)}, u32[]{:S(2)}) copy-start(bf16[8,128,128]{2,1,0:T(8,128)(2,1)} %param.11) | copy-start | bytes 786436
  0.0 5.9 %copy-start.1 = (bf16[8,128,128]{2,1,0:T(8,128)(2,1)S(1)}, bf16[8,128,128]{2,1,0:T(8,128)(2,1)}, u32[]{:S(2)}) copy-start(bf16[8,128,128]{2,1,0:T(8,128)(2,1)} %param.12) | copy-start | bytes 786436
  0.0 7.3 %copy-start.5 = (s32[4,12]{1,0:T(4,128)S(1)}, s32[4,12]{1,0:T(4,128)}, u32[]{:S(2)}) copy-start(s32[4,12]{1,0:T(4,128)} %param.14) | copy-start | bytes 580
  10.0 4.8 %copy-start.2 = (bf16[12,128,128]{2,1,0:T(8,128)(2,1)S(1)}, bf16[12,128,128]{2,1,0:T(8,128)(2,1)}, u32[]{:S(2)}) copy-start(bf16[12,128,128]{2,1,0:T(8,128)(2,1)} %gather_fusion.2) | copy-start | bytes 1179652
  46.5 23.8 %copy-start.3 = (bf16[4,2,128,128]{3,2,1,0:T(8,128)(2,1)S(1)}, bf16[4,2,128,128]{3,2,1,0:T(8,128)(2,1)}, u32[]{:S(2)}) copy-start(bf16[4,2,128,128]{3,2,1,0:T(8,128)(2,1)} %param.17) | copy-start | bytes 786436
  46.5 24.0 %copy-start.4 = (bf16[4,2,128,128]{3,2,1,0:T(8,128)(2,1)S(1)}, bf16[4,2,128,128]{3,2,1,0:T(8,128)(2,1)}, u32[]{:S(2)}) copy-start(bf16[4,2,128,128]{3,2,1,0:T(8,128)(2,1)} %param.16) | copy-start | bytes 786436
  48.1 30.6 %collective-permute-start = (bf16[4,2,3,128,128]{4,0,3,2,1:T(4,128)(2,1)S(1)}, bf16[4,2,3,128,128]{4,0,3,2,1:T(4,128)(2,1)S(1)}, u32[]{:S(2)}, u32[]{:S(2)}) collective-permute-start(bf16[4,2,3,128,128]{4,0,3,2,1:T(4,128)(2,1)S(1)} %get-tuple-element.24), channel_id=1, source_target_pairs={{0,504},{4,508},{8,0},{12,4},{16,8},{20,12},{24,16},{28,20},{32,24... | collective-permute-start | bytes 2359304 | tf_op jit(solution)/shard_map/ppermute | solution.py:12
  62.5 16.2 %collective-permute-start.1 = (bf16[4,2,3,128,128]{4,0,3,2,1:T(4,128)(2,1)S(1)}, bf16[4,2,3,128,128]{4,0,3,2,1:T(4,128)(2,1)S(1)}, u32[]{:S(2)}, u32[]{:S(2)}) collective-permute-start(bf16[4,2,3,128,128]{4,0,3,2,1:T(4,128)(2,1)S(1)} %get-tuple-element.27), channel_id=1, source_target_pairs={{0,508},{4,0},{8,4},{12,8},{16,12},{20,16},{24,20},{28,24},{32,28}... | collective-permute-start | bytes 2359304 | tf_op jit(solution)/shard_map/ppermute | solution.py:12
  65.4 17.5 %collective-permute-start.2 = (bf16[4,2,3,128,128]{4,0,3,2,1:T(4,128)(2,1)S(1)}, bf16[4,2,3,128,128]{4,0,3,2,1:T(4,128)(2,1)S(1)}, u32[]{:S(2)}, u32[]{:S(2)}) collective-permute-start(bf16[4,2,3,128,128]{4,0,3,2,1:T(4,128)(2,1)S(1)} %get-tuple-element.26), channel_id=1, source_target_pairs={{0,4},{4,8},{8,12},{12,16},{16,20},{20,24},{24,28},{28,32},{32,36}... | collective-permute-start | bytes 2359304 | tf_op jit(solution)/shard_map/ppermute | solution.py:12
  68.1 30.6 %collective-permute-start.3 = (bf16[4,2,3,128,128]{4,0,3,2,1:T(4,128)(2,1)S(1)}, bf16[4,2,3,128,128]{4,0,3,2,1:T(4,128)(2,1)S(1)}, u32[]{:S(2)}, u32[]{:S(2)}) collective-permute-start(bf16[4,2,3,128,128]{4,0,3,2,1:T(4,128)(2,1)S(1)} %get-tuple-element.25), channel_id=1, source_target_pairs={{0,8},{4,12},{8,16},{12,20},{16,24},{20,28},{24,32},{28,36},{32,40... | collective-permute-start | bytes 2359304 | tf_op jit(solution)/shard_map/ppermute | solution.py:12
  100.1 7.8 %collective-permute-start.4 = (bf16[4,3,128,128]{3,0,2,1:T(4,128)(2,1)S(1)}, bf16[4,3,128,128]{3,0,2,1:T(4,128)(2,1)S(1)}, u32[]{:S(2)}, u32[]{:S(2)}) collective-permute-start(bf16[4,3,128,128]{3,0,2,1:T(4,128)(2,1)S(1)} %fusion.41), channel_id=1, source_target_pairs={{0,1},{1,2},{2,3},{4,5},{5,6},{6,7},{8,9},{9,10},{10,11},{12,13},{... | collective-permute-start | bytes 1179656 | tf_op jit(solution)/shard_map/ppermute | solution.py:18
  103.4 8.5 %collective-permute-start.5 = (bf16[4,3,128,128]{3,0,2,1:T(4,128)(2,1)S(1)}, bf16[4,3,128,128]{3,0,2,1:T(4,128)(2,1)S(1)}, u32[]{:S(2)}, u32[]{:S(2)}) collective-permute-start(bf16[4,3,128,128]{3,0,2,1:T(4,128)(2,1)S(1)} %fusion.42), channel_id=1, source_target_pairs={{1,0},{2,1},{3,2},{5,4},{6,5},{7,6},{9,8},{10,9},{11,10},{13,12},{... | collective-permute-start | bytes 1179656 | tf_op jit(solution)/shard_map/ppermute | solution.py:18
where the time goes:
time: 114 us
  matrix products  35.8 us (31%)
  waiting for transfers between devices  34.7 us (30%)
  starting transfers between devices  26.5 us (23%)
  local copies, waits for them, and re-layouts  12.7 us (11%)
  other arithmetic  3.87 us (3%)
    ppermute x4, waiting for transfers between devices, from_behind(): return lax.ppermute(value, axis, pairs)  28 us
    dot_general x4, matrix products, slot_terms(): jnp.einsum('kw,klfbd->wlfbd', pick_table, slot_part, preferred_element_ty...  25.4 us
    ppermute x4, starting transfers between devices, from_behind(): return lax.ppermute(value, axis, pairs)  22.1 us
    dot_general x4, matrix products, slot_terms(): jnp.einsum('klfbc,kcd->klfbd', lat_applied, lon_sel, preferred_element_ty...  10.4 us
    ppermute x2, waiting for transfers between devices, passed_along(): return lax.ppermute(x, axis, pairs)  6.61 us
    gather x4, local copies, waits for them, and re-layouts, per_device(): lon_sel = jnp.take(lon_weights, blocks[tile_pos, :, 1], axis=0)  5.65 us
    ppermute x2, starting transfers between devices, passed_along(): return lax.ppermute(x, axis, pairs)  4.43 us
    gather x4, local copies, waits for them, and re-layouts, per_device(): lat_sel = jnp.take(lat_weights, blocks[tile_pos, :, 0], axis=0)  3.21 us
  transfers between devices with their start and end apart: 6, of which 5 were waited for; matrix products, arithmetic and copies ran while one was open for 1% of the time, Pallas kernels for 0%

commit v1 on v0

v1 whole, which is shorter than its diff:
```python
import jax
import jax.numpy as jnp
from jax import lax
from jax.experimental import pallas as pl
from jax.experimental.pallas import tpu as pltpu
from jax.sharding import PartitionSpec as P

REACH = 2
DEAD = 64
VMEM = pl.BlockSpec(memory_space=pltpu.VMEM)
SMEM = pl.BlockSpec(memory_space=pltpu.SMEM)


def gather_slots(meta_ref, where, tiles, slots, first, code_list, block_list, base):
    n = base
    for t in range(tiles):
        for k in range(slots):
            i = t * slots + k
            s = meta_ref[0, i] - first
            hit = jnp.logical_and(s >= 0, s < tiles)
            code_list[n] = s * (2 * tiles) + (where * tiles + t)
            block_list[n] = meta_ref[1, i]
            n = n + hit.astype(jnp.int32)
    return n


def add_slots(n, source_refs, tiles, planes, size, code_list, block_list, lat_t_ref, lon_ref, acc_ref):
    rows = planes * size
    code_list[n] = tiles * (2 * tiles)
    block_list[n] = 0

    def one(i):
        code = code_list[i]
        blk = block_list[i]
        s = code // (2 * tiles)
        t = code % (2 * tiles)
        lat_t = lat_t_ref[blk // 8]
        lon = lon_ref[blk % 8]
        return s, t, lat_t, lon

    def part(ref, t, lat_t):
        a = ref[pl.ds(pl.multiple_of(t * rows, rows), rows), :]
        outs = []
        for j in range(0, planes, 2):
            pair = jnp.concatenate(
                [a[j * size : (j + 1) * size], a[(j + 1) * size : (j + 2) * size]], axis=1
            )
            p = jnp.dot(lat_t, pair, preferred_element_type=jnp.float32).astype(jnp.bfloat16)
            outs += [p[:, :size], p[:, size:]]
        return jnp.concatenate(outs, axis=0)

    (ref,) = source_refs

    def body(i, carry):
        s0, t0, lt0, ln0 = one(2 * i)
        s1, t1, lt1, ln1 = one(2 * i + 1)
        p0 = part(ref, t0, lt0)
        p1 = part(ref, t1, lt1)
        q0 = jnp.dot(p0, ln0, preferred_element_type=jnp.float32)
        q1 = jnp.dot(p1, ln1, preferred_element_type=jnp.float32)
        acc_ref[s0] += q0
        acc_ref[s1] += q1
        return carry

    lax.fori_loop(0, (n + 1) // 2, body, 0)


def phase(source, meta, shift, lat_t, lon, acc, tiles, slots, planes, size):
    def kernel(*refs):
        if acc is None:
            shift_ref, meta_ref, src, lat_ref, lon_ref, out_ref, code_list, block_list = refs
            out_ref[...] = jnp.zeros_like(out_ref)
        else:
            shift_ref, meta_ref, src, lat_ref, lon_ref, acc_ref, out_ref, code_list, block_list = refs
        n = gather_slots(meta_ref, 0, tiles, slots, shift_ref[0], code_list, block_list, 0)
        add_slots(n, (src,), tiles, planes, size, code_list, block_list, lat_ref, lon_ref, out_ref)

    args = [shift, meta, source, lat_t, lon]
    specs = [SMEM, SMEM, VMEM, VMEM, VMEM]
    if acc is not None:
        args.append(acc)
        specs.append(VMEM)
    return pl.pallas_call(
        kernel,
        out_shape=jax.ShapeDtypeStruct((tiles + 1, planes * size, size), jnp.float32),
        in_specs=specs,
        out_specs=VMEM,
        scratch_shapes=[
            pltpu.SMEM((tiles * slots + 2,), jnp.int32),
            pltpu.SMEM((tiles * slots + 2,), jnp.int32),
        ],
        input_output_aliases={} if acc is None else {5: 0},
        compiler_params=pltpu.CompilerParams(vmem_limit_bytes=40 << 20),
    )(*args)


def flows(acc, upper, lower, tiles, levels, fields, size):
    def kernel(acc_ref, upper_ref, lower_ref, up_ref, down_ref):
        for s in range(tiles):
            u = upper_ref[s, levels - 1].astype(jnp.float32)
            d = lower_ref[s, 0].astype(jnp.float32)
            for f in range(fields):
                top = ((levels - 1) * fields + f) * size
                up_ref[s, f] = (u * acc_ref[s, top : top + size]).astype(jnp.bfloat16)
                down_ref[s, f] = (d * acc_ref[s, f * size : (f + 1) * size]).astype(jnp.bfloat16)

    rim = jax.ShapeDtypeStruct((tiles, fields, size, size), jnp.bfloat16)
    return pl.pallas_call(
        kernel,
        out_shape=(rim, rim),
        in_specs=[VMEM] * 3,
        out_specs=(VMEM, VMEM),
        compiler_params=pltpu.CompilerParams(vmem_limit_bytes=40 << 20),
    )(acc, upper, lower)


def couple(acc, upper, lower, rim_low, rim_up, tiles, levels, fields, size):
    def kernel(acc_ref, upper_ref, lower_ref, low_ref, up_ref, out_ref):
        us = [upper_ref[0, l].astype(jnp.float32) for l in range(levels)]
        ds = [lower_ref[0, l].astype(jnp.float32) for l in range(levels)]
        for f in range(fields):
            v = [acc_ref[0, (l * fields + f) * size : (l * fields + f + 1) * size] for l in range(levels)]
            for l in range(levels):
                below = low_ref[0, f].astype(jnp.float32) if l == 0 else us[l - 1] * v[l - 1]
                above = up_ref[0, f].astype(jnp.float32) if l == levels - 1 else ds[l + 1] * v[l + 1]
                out_ref[0, l, f] = ((1.0 + us[l] + ds[l]) * v[l] - below - above).astype(jnp.bfloat16)

    coef = pl.BlockSpec((1, levels, size, size), lambda s: (s, 0, 0, 0))
    rim = pl.BlockSpec((1, fields, size, size), lambda s: (s, 0, 0, 0))
    return pl.pallas_call(
        kernel,
        grid=(tiles,),
        out_shape=jax.ShapeDtypeStruct((tiles, levels, fields, size, size), jnp.bfloat16),
        in_specs=[
            pl.BlockSpec((1, levels * fields * size, size), lambda s: (s, 0, 0)),
            coef,
            coef,
            rim,
            rim,
        ],
        out_specs=pl.BlockSpec((1, levels, fields, size, size), lambda s: (s, 0, 0, 0, 0)),
        compiler_params=pltpu.CompilerParams(vmem_limit_bytes=40 << 20),
    )(acc, upper, lower, rim_low, rim_up)


def passed_along(x, axis, by):
    length = lax.axis_size(axis)
    pairs = [(i, i + by) for i in range(length) if 0 <= i + by < length]
    return lax.ppermute(x, axis, pairs)


def per_device(
    adj_out, lat_weights, lon_weights, counts, departures, blocks, upper_coef, lower_coef
):
    tile_devices = lax.axis_size("tile")
    own_index = lax.axis_index("tile")
    tiles, slots = departures.shape
    levels, fields, size = adj_out.shape[1], adj_out.shape[2], adj_out.shape[3]
    planes = levels * fields
    rows = tiles * planes * size
    base_tile = (own_index - REACH) % tile_devices * tiles
    window_row = (departures - base_tile) % (tile_devices * tiles)
    live = jnp.arange(slots, dtype=jnp.int32)[None, :] < counts[:, None]
    meta = jnp.stack(
        [
            jnp.where(live, window_row, DEAD).reshape(-1),
            (blocks[:, :, 0] * 8 + blocks[:, :, 1]).reshape(-1),
        ]
    )
    flat = adj_out.reshape(rows, size)
    tail = jnp.pad(meta.astype(jnp.bfloat16), ((0, 14), (0, size - tiles * slots)))
    packed = jnp.concatenate([flat, tail], axis=0)

    def unpack_meta(arrived):
        return arrived[rows : rows + 2, : tiles * slots].astype(jnp.int32)

    def permuted(x, even_by, odd_by):
        pairs = [(i, (i + (even_by if i % 2 == 0 else odd_by)) % tile_devices) for i in range(tile_devices)]
        return lax.ppermute(x, "tile", pairs)

    odd = own_index % 2
    sign = 1 - 2 * odd

    def shift(offset):
        return ((REACH - offset) * tiles).reshape(1).astype(jnp.int32)

    lat_t = jnp.swapaxes(lat_weights, 1, 2)
    x_in = permuted(packed, -2, 2)
    mate = permuted(packed, 1, -1)

    def step(source, source_meta, offset, acc):
        return phase(source, source_meta, shift(offset), lat_t, lon_weights, acc, tiles, slots, planes, size)

    acc = step(flat, meta, 0 * sign, None)
    packed_y, acc = lax.optimization_barrier((packed, acc))
    y_in = permuted(packed_y, 2, -2)
    acc = step(mate, unpack_meta(mate), sign, acc)
    x_mate = permuted(x_in, 1, -1)
    acc = step(x_in, unpack_meta(x_in), 2 * sign, acc)
    acc = step(x_mate, unpack_meta(x_mate), -sign, acc)
    acc = step(y_in, unpack_meta(y_in), -2 * sign, acc)
    up, down = flows(acc, upper_coef, lower_coef, tiles, levels, fields, size)
    rim_low = passed_along(up, "lev", 1)
    rim_up = passed_along(down, "lev", -1)
    return couple(acc, upper_coef, lower_coef, rim_low, rim_up, tiles, levels, fields, size)


def solution(mesh):
    placed = (
        P("tile", "lev", None, None, None),
        P(),
        P(),
        P("tile"),
        P("tile", None),
        P("tile", None, None),
        P("tile", "lev", None, None),
        P("tile", "lev", None, None),
    )
    return jax.shard_map(
        per_device,
        mesh=mesh,
        in_specs=placed,
        out_specs=P("tile", "lev", None, None, None),
        check_vma=False,
    )
```

time: 114 us -> 62.3 us (0.55)
  the two profiles are of different devices: /device:TPU:1 before, /device:TPU:2 now
where the time goes in v1:
time: 62.3 us; the launch traced here: 61.7 us
  starting transfers between devices  25.5 us (41%)
  waiting for transfers between devices  17.9 us (29%)
  Pallas kernels  11.2 us (18%)
  other arithmetic  5.74 us (9%)
  local copies, waits for them, and re-layouts  1.31 us (2%)
    ppermute x4, starting transfers between devices, permuted(): return lax.ppermute(x, 'tile', pairs)  19.6 us
    ppermute x2, waiting for transfers between devices, passed_along(): return lax.ppermute(x, axis, pairs)  9.63 us
    pallas_call x5, Pallas kernels, phase(): pl.pallas_call(kernel, out_shape=jax.ShapeDtypeStruct((tiles + 1, planes...  9.46 us
    ppermute x4, waiting for transfers between devices, permuted(): return lax.ppermute(x, 'tile', pairs)  8.23 us
    ppermute x2, starting transfers between devices, passed_along(): return lax.ppermute(x, axis, pairs)  5.86 us
    concatenate x1, other arithmetic, per_device(): packed = jnp.concatenate([flat, tail], axis=0)  2.07 us
    convert_element_type x4, other arithmetic, unpack_meta(): return arrived[rows:rows + 2, :tiles * slots].astype(jnp.int32)  2.03 us
    pallas_call x1, Pallas kernels, couple(): pl.pallas_call(kernel, grid=(tiles,), out_shape=jax.ShapeDtypeStruct((til...  1.64 us
  transfers between devices with their start and end apart: 6, of which 4 were waited for; matrix products, arithmetic and copies ran while one was open for 4% of the time, Pallas kernels for 9%

profile of v1, /device:TPU:2, one launch (start us, length us, event | category | flops | bytes accessed | tf_op | source)
XLA Modules:
  0.0 61.7 jit_solution(1237413567874444051)
XLA Ops:
  0.0 0.8 %fusion.3 = s32[4,12]{1,0:T(4,128)S(1)} fusion(s32[4,12]{1,0:T(4,128)} %param.12, s32[]{:T(128)S(6)} %mul.37, s32[4]{0:T(128)} %param.11), kind=kLoop, calls=%fused_computation.7 | loop fusion | flops 672 | bytes 404 | tf_op jit(solution)/shard_map/jit(_where)/select_n | solution.py:166
  0.8 0.1 stack_reshape.4
  0.9 0.8 %add_reduce_fusion = s32[4,12]{1,0:T(4,128)S(1)} fusion(s32[4,12,2]{1,2,0:T(2,128)} %param.13), kind=kLoop, calls=%fused_computation.8 | loop fusion | flops 96 | bytes 576 | tf_op jit(solution)/shard_map/add | solution.py:167
  1.7 0.1 add.33
  1.8 2.1 %fusion.1 = bf16[3088,128]{1,0:T(8,128)(2,1)} fusion(bf16[2,48]{1,0:T(2,128)(2,1)S(1)} %get-tuple-element.14, bf16[3072,128]{1,0:T(8,128)(2,1)} %bitcast.11), kind=kLoop, calls=%fused_computation.2 | loop fusion | flops 2371584 | bytes 1577152 | tf_op jit(solution)/shard_map/concatenate | solution.py:172
  3.9 13.8 %collective-permute-start.1 = (bf16[3088,128]{1,0:T(8,128)(2,1)}, bf16[3088,128]{1,0:T(8,128)(2,1)}, u32[]{:S(2)}, u32[]{:S(2)}) collective-permute-start(bf16[3088,128]{1,0:T(8,128)(2,1)} %fusion.1), channel_id=1, source_target_pairs={{0,504},{4,12},{8,0},{12,20},{16,8},{20,28},{24,16},{28,36},{32,24... | collective-permute-start | bytes 2371592 | tf_op jit(solution)/shard_map/ppermute | solution.py:179
  17.7 1.9 %collective-permute-start.3 = (bf16[3088,128]{1,0:T(8,128)(2,1)}, bf16[3088,128]{1,0:T(8,128)(2,1)}, u32[]{:S(2)}, u32[]{:S(2)}) collective-permute-start(bf16[3088,128]{1,0:T(8,128)(2,1)} %fusion.1), channel_id=1, source_target_pairs={{0,4},{4,0},{8,12},{12,8},{16,20},{20,16},{24,28},{28,24},{32,36},... | collective-permute-start | bytes 2371592 | tf_op jit(solution)/shard_map/ppermute | solution.py:179
  19.7 1.1 %copy.14 = bf16[8,128,128]{1,2,0:T(8,128)(2,1)S(1)} copy(bf16[8,128,128]{2,1,0:T(8,128)(2,1)} %param.9) | data formatting | bytes 524288 | tf_op args[1]
  20.8 0.0 copy-done.1
  20.8 0.0 copy-done
  20.8 1.6 %shard_map.82.refs_5_ = f32[5,768,128]{2,1,0:T(8,128)S(1)} custom-call(s32[1]{0:T(128)} %constant.57.clone.1.refs_0_, s32[2,48]{1,0:T(2,128)S(1)} %get-tuple-element.13.refs_1_, bf16[3072,128]{1,0:T(8,128)(2,1)S(1)} %bitcast.12, bf16[8,128,128]{2,1,0:T(8,128)(2,1)S(1)} %bitcast.6, bf16[8,128,128]{2,1,0:T(8,128)(2,1)S(1)} %copy-done), custom_call_target="tpu_custom_call" | custom-call | tf_op jit(solution)/shard_map/pallas_call | solution.py:83
  22.4 1.9 %collective-permute-start = (bf16[3088,128]{1,0:T(8,128)(2,1)}, bf16[3088,128]{1,0:T(8,128)(2,1)S(1)}, u32[]{:S(2)}, u32[]{:S(2)}) collective-permute-start(bf16[3088,128]{1,0:T(8,128)(2,1)} %fusion.1), channel_id=1, source_target_pairs={{0,8},{4,508},{8,16},{12,4},{16,24},{20,12},{24,32},{28,20},{32,40... | collective-permute-start | bytes 2371592 | tf_op jit(solution)/shard_map/ppermute | solution.py:179
  24.4 4.6 %collective-permute-done.1.refs_2_ = bf16[3088,128]{1,0:T(8,128)(2,1)} collective-permute-done((bf16[3088,128]{1,0:T(8,128)(2,1)}, bf16[3088,128]{1,0:T(8,128)(2,1)}, u32[]{:S(2)}, u32[]{:S(2)}) %collective-permute-start.1) | collective-permute-done | bytes 790560 | tf_op jit(solution)/shard_map/ppermute | solution.py:179
  28.9 1.9 %collective-permute-start.2 = (bf16[3088,128]{1,0:T(8,128)(2,1)}, bf16[3088,128]{1,0:T(8,128)(2,1)}, u32[]{:S(2)}, u32[]{:S(2)}) collective-permute-start(bf16[3088,128]{1,0:T(8,128)(2,1)} %collective-permute-done.1.refs_2_), channel_id=1, source_target_pairs={{0,4},{4,0},{8,12},{12,8},{16,20},{20,16},{24,28},{28,24},{32,36},... | collective-permute-start | bytes 2371592 | tf_op jit(solution)/shard_map/ppermute | solution.py:179
  30.9 0.0 collective-permute-done.3.refs_2_
  30.9 0.7 %slice_convert_fusion.refs_1_ = s32[2,48]{1,0:T(2,128)S(1)} fusion(bf16[3088,128]{1,0:T(8,128)(2,1)} %collective-permute-done.3.refs_2_), kind=kLoop, calls=%fused_computation.11 | loop fusion | flops 96 | bytes 576 | tf_op jit(solution)/shard_map/convert_element_type | solution.py:175
  31.5 2.2 %shard_map.83.refs_5_ = f32[5,768,128]{2,1,0:T(8,128)S(1)} custom-call(s32[1]{0:T(128)} %bitcast.5.refs_0_, s32[2,48]{1,0:T(2,128)S(1)} %slice_convert_fusion.refs_1_, bf16[3088,128]{1,0:T(8,128)(2,1)} %collective-permute-done.3.refs_2_, bf16[8,128,128]{2,1,0:T(8,128)(2,1)S(1)} %bitcast.7, ...), custom_call_target="tpu_custom_call", output_to_operand_aliasing={{}: (5, {})} | custom-call | tf_op jit(solution)/shard_map/pallas_call | solution.py:83
  33.8 0.7 %slice_convert_fusion.1.refs_1_ = s32[2,48]{1,0:T(2,128)S(1)} fusion(bf16[3088,128]{1,0:T(8,128)(2,1)} %collective-permute-done.1.refs_2_), kind=kLoop, calls=%fused_computation.12 | loop fusion | flops 96 | bytes 576 | tf_op jit(solution)/shard_map/convert_element_type | solution.py:175
  34.4 1.8 %shard_map.84.refs_5_ = f32[5,768,128]{2,1,0:T(8,128)S(1)} custom-call(s32[1]{0:T(128)} %bitcast.4.refs_0_, s32[2,48]{1,0:T(2,128)S(1)} %slice_convert_fusion.1.refs_1_, bf16[3088,128]{1,0:T(8,128)(2,1)} %collective-permute-done.1.refs_2_, bf16[8,128,128]{2,1,0:T(8,128)(2,1)S(1)} %bitcast.8, ...), custom_call_target="tpu_custom_call", output_to_operand_aliasing={{}: (5, {})} | custom-call | tf_op jit(solution)/shard_map/pallas_call | solution.py:83
  36.2 3.7 %collective-permute-done.refs_2_ = bf16[3088,128]{1,0:T(8,128)(2,1)S(1)} collective-permute-done((bf16[3088,128]{1,0:T(8,128)(2,1)}, bf16[3088,128]{1,0:T(8,128)(2,1)S(1)}, u32[]{:S(2)}, u32[]{:S(2)}) %collective-permute-start) | collective-permute-done | bytes 790560 | tf_op jit(solution)/shard_map/ppermute | solution.py:179
  39.9 0.0 collective-permute-done.2.refs_2_
  39.9 0.7 %slice_convert_fusion.2.refs_1_ = s32[2,48]{1,0:T(2,128)S(1)} fusion(bf16[3088,128]{1,0:T(8,128)(2,1)} %collective-permute-done.2.refs_2_), kind=kLoop, calls=%fused_computation.13 | loop fusion | flops 96 | bytes 576 | tf_op jit(solution)/shard_map/convert_element_type | solution.py:175
  40.6 2.2 %shard_map.85.refs_5_ = f32[5,768,128]{2,1,0:T(8,128)S(1)} custom-call(s32[1]{0:T(128)} %bitcast.3.refs_0_, s32[2,48]{1,0:T(2,128)S(1)} %slice_convert_fusion.2.refs_1_, bf16[3088,128]{1,0:T(8,128)(2,1)} %collective-permute-done.2.refs_2_, bf16[8,128,128]{2,1,0:T(8,128)(2,1)S(1)} %bitcast.9, ...), custom_call_target="tpu_custom_call", output_to_operand_aliasing={{}: (5, {})} | custom-call | tf_op jit(solution)/shard_map/pallas_call | solution.py:83
  42.8 0.0 copy-start.2
  42.8 0.0 copy-start.3
  42.8 1.6 %shard_map.86.acc_ref = f32[5,768,128]{2,1,0:T(8,128)S(1)} custom-call(s32[1]{0:T(128)} %bitcast.refs_0_, s32[2,48]{1,0:T(2,128)S(1)} %slice_convert_fusion.3.refs_1_, bf16[3088,128]{1,0:T(8,128)(2,1)S(1)} %collective-permute-done.refs_2_, bf16[8,128,128]{2,1,0:T(8,128)(2,1)S(1)} %bitcast.10, ...), custom_call_target="tpu_custom_call", output_to_operand_aliasing={{}: (5, {})} | custom-call | tf_op jit(solution)/shard_map/pallas_call | solution.py:83
  44.5 0.1 shard_map.87
  44.6 3.4 %collective-permute-start.4 = (bf16[4,3,128,128]{3,2,1,0:T(8,128)(2,1)S(1)}, bf16[4,3,128,128]{3,2,1,0:T(8,128)(2,1)S(1)}, u32[]{:S(2)}, u32[]{:S(2)}) collective-permute-start(bf16[4,3,128,128]{3,2,1,0:T(8,128)(2,1)S(1)} %get-tuple-element.11), channel_id=1, source_target_pairs={{0,1},{1,2},{2,3},{4,5},{5,6},{6,7},{8,9},{9,10},{10,11},{12,13},{... | collective-permute-start | bytes 1179656 | tf_op jit(solution)/shard_map/ppermute | solution.py:149
  48.0 2.5 %collective-permute-start.5 = (bf16[4,3,128,128]{3,2,1,0:T(8,128)(2,1)S(1)}, bf16[4,3,128,128]{3,2,1,0:T(8,128)(2,1)S(1)}, u32[]{:S(2)}, u32[]{:S(2)}) collective-permute-start(bf16[4,3,128,128]{3,2,1,0:T(8,128)(2,1)S(1)} %get-tuple-element.12), channel_id=1, source_target_pairs={{1,0},{2,1},{3,2},{5,4},{6,5},{7,6},{9,8},{10,9},{11,10},{13,12},{... | collective-permute-start | bytes 1179656 | tf_op jit(solution)/shard_map/ppermute | solution.py:149
  50.5 6.5 %collective-permute-done.4.low_ref = bf16[4,3,128,128]{3,2,1,0:T(8,128)(2,1)S(1)} collective-permute-done((bf16[4,3,128,128]{3,2,1,0:T(8,128)(2,1)S(1)}, bf16[4,3,128,128]{3,2,1,0:T(8,128)(2,1)S(1)}, u32[]{:S(2)}, u32[]{:S(2)}) %collective-permute-start.4) | collective-permute-done | bytes 393248 | tf_op jit(solution)/shard_map/ppermute | solution.py:149
  57.0 3.1 %collective-permute-done.5.up_ref = bf16[4,3,128,128]{3,2,1,0:T(8,128)(2,1)S(1)} collective-permute-done((bf16[4,3,128,128]{3,2,1,0:T(8,128)(2,1)S(1)}, bf16[4,3,128,128]{3,2,1,0:T(8,128)(2,1)S(1)}, u32[]{:S(2)}, u32[]{:S(2)}) %collective-permute-start.5) | collective-permute-done | bytes 393248 | tf_op jit(solution)/shard_map/ppermute | solution.py:149
  60.1 1.6 %shard_map.88 = bf16[4,2,3,128,128]{4,3,2,1,0:T(8,128)(2,1)} custom-call(f32[5,768,128]{2,1,0:T(8,128)S(1)} %shard_map.86.acc_ref, bf16[4,2,128,128]{3,2,1,0:T(8,128)(2,1)S(1)} %copy-done.2, bf16[4,2,128,128]{3,2,1,0:T(8,128)(2,1)S(1)} %copy-done.3, bf16[4,3,128,128]{3,2,1,0:T(8,128)(2,1)S(1)} %collective-permute-done.4.low_ref, ...), custom_call_target="tpu_custom_call" | custom-call | tf_op jit(solution)/shard_map/pallas_call | solution.py:130
  (6 shorter events, 0.0 us)
Async XLA Ops:
  0.0 20.8 %copy-start.1 = (bf16[4,2,3,128,128]{4,3,2,1,0:T(8,128)(2,1)S(1)}, bf16[4,2,3,128,128]{4,3,2,1,0:T(8,128)(2,1)}, u32[]{:S(2)}) copy-start(bf16[4,2,3,128,128]{4,3,2,1,0:T(8,128)(2,1)} %param.8) | copy-start | bytes 2359300
  0.0 20.8 %copy-start = (bf16[8,128,128]{2,1,0:T(8,128)(2,1)S(1)}, bf16[8,128,128]{2,1,0:T(8,128)(2,1)}, u32[]{:S(2)}) copy-start(bf16[8,128,128]{2,1,0:T(8,128)(2,1)} %refs_4_.9) | copy-start | bytes 786436
  3.9 25.0 %collective-permute-start.1 = (bf16[3088,128]{1,0:T(8,128)(2,1)}, bf16[3088,128]{1,0:T(8,128)(2,1)}, u32[]{:S(2)}, u32[]{:S(2)}) collective-permute-start(bf16[3088,128]{1,0:T(8,128)(2,1)} %fusion.1), channel_id=1, source_target_pairs={{0,504},{4,12},{8,0},{12,20},{16,8},{20,28},{24,16},{28,36},{32,24... | collective-permute-start | bytes 2371592 | tf_op jit(solution)/shard_map/ppermute | solution.py:179
  17.7 13.1 %collective-permute-start.3 = (bf16[3088,128]{1,0:T(8,128)(2,1)}, bf16[3088,128]{1,0:T(8,128)(2,1)}, u32[]{:S(2)}, u32[]{:S(2)}) collective-permute-start(bf16[3088,128]{1,0:T(8,128)(2,1)} %fusion.1), channel_id=1, source_target_pairs={{0,4},{4,0},{8,12},{12,8},{16,20},{20,16},{24,28},{28,24},{32,36},... | collective-permute-start | bytes 2371592 | tf_op jit(solution)/shard_map/ppermute | solution.py:179
  22.4 17.5 %collective-permute-start = (bf16[3088,128]{1,0:T(8,128)(2,1)}, bf16[3088,128]{1,0:T(8,128)(2,1)S(1)}, u32[]{:S(2)}, u32[]{:S(2)}) collective-permute-start(bf16[3088,128]{1,0:T(8,128)(2,1)} %fusion.1), channel_id=1, source_target_pairs={{0,8},{4,508},{8,16},{12,4},{16,24},{20,12},{24,32},{28,20},{32,40... | collective-permute-start | bytes 2371592 | tf_op jit(solution)/shard_map/ppermute | solution.py:179
  28.9 11.0 %collective-permute-start.2 = (bf16[3088,128]{1,0:T(8,128)(2,1)}, bf16[3088,128]{1,0:T(8,128)(2,1)}, u32[]{:S(2)}, u32[]{:S(2)}) collective-permute-start(bf16[3088,128]{1,0:T(8,128)(2,1)} %collective-permute-done.1.refs_2_), channel_id=1, source_target_pairs={{0,4},{4,0},{8,12},{12,8},{16,20},{20,16},{24,28},{28,24},{32,36},... | collective-permute-start | bytes 2371592 | tf_op jit(solution)/shard_map/ppermute | solution.py:179
  42.8 1.7 %copy-start.2 = (bf16[4,2,128,128]{3,2,1,0:T(8,128)(2,1)S(1)}, bf16[4,2,128,128]{3,2,1,0:T(8,128)(2,1)}, u32[]{:S(2)}) copy-start(bf16[4,2,128,128]{3,2,1,0:T(8,128)(2,1)} %upper_ref.3) | copy-start | bytes 786436
  42.8 1.7 %copy-start.3 = (bf16[4,2,128,128]{3,2,1,0:T(8,128)(2,1)S(1)}, bf16[4,2,128,128]{3,2,1,0:T(8,128)(2,1)}, u32[]{:S(2)}) copy-start(bf16[4,2,128,128]{3,2,1,0:T(8,128)(2,1)} %lower_ref.3) | copy-start | bytes 786436
  44.6 12.4 %collective-permute-start.4 = (bf16[4,3,128,128]{3,2,1,0:T(8,128)(2,1)S(1)}, bf16[4,3,128,128]{3,2,1,0:T(8,128)(2,1)S(1)}, u32[]{:S(2)}, u32[]{:S(2)}) collective-permute-start(bf16[4,3,128,128]{3,2,1,0:T(8,128)(2,1)S(1)} %get-tuple-element.11), channel_id=1, source_target_pairs={{0,1},{1,2},{2,3},{4,5},{5,6},{6,7},{8,9},{9,10},{10,11},{12,13},{... | collective-permute-start | bytes 1179656 | tf_op jit(solution)/shard_map/ppermute | solution.py:149
  48.0 12.1 %collective-permute-start.5 = (bf16[4,3,128,128]{3,2,1,0:T(8,128)(2,1)S(1)}, bf16[4,3,128,128]{3,2,1,0:T(8,128)(2,1)S(1)}, u32[]{:S(2)}, u32[]{:S(2)}) collective-permute-start(bf16[4,3,128,128]{3,2,1,0:T(8,128)(2,1)S(1)} %get-tuple-element.12), channel_id=1, source_target_pairs={{1,0},{2,1},{3,2},{5,4},{6,5},{7,6},{9,8},{10,9},{11,10},{13,12},{... | collective-permute-start | bytes 1179656 | tf_op jit(solution)/shard_map/ppermute | solution.py:149

commit v2 on v0

v2 whole, which is shorter than its diff:
```python
import jax
import jax.numpy as jnp
from jax import lax
from jax.experimental import pallas as pl
from jax.experimental.pallas import tpu as pltpu
from jax.sharding import PartitionSpec as P

REACH = 2
DEAD = 64
META = 16
O_FLOPS = 1 << 0
M_FLOPS = 1 << 36
XM_FLOPS = 1 << 0
L_FLOPS = 1 << 0
VMEM = pl.BlockSpec(memory_space=pltpu.VMEM)
SMEM = pl.BlockSpec(memory_space=pltpu.SMEM)
HBM = pl.BlockSpec(memory_space=pltpu.HBM)
COST = pl.CostEstimate(flops=1, transcendentals=0, bytes_accessed=1)
PARAMS = pltpu.CompilerParams(vmem_limit_bytes=6 << 20)


def in_hbm(x):
    return pltpu.with_memory_space_constraint(x, pltpu.HBM)


def pack(flat, counts, departures, blocks, base):
    rows, size = flat.shape
    tiles, slots = departures.shape
    wrap = lax.axis_size("tile") * tiles

    def kernel(base_ref, counts_hbm, dep_hbm, blk_hbm, flat_hbm, out_hbm, counts_ref, dep, blk, meta, tail, body, sems):
        copies = [
            pltpu.make_async_copy(counts_hbm, counts_ref, sems.at[0]),
            pltpu.make_async_copy(dep_hbm, dep, sems.at[1]),
            pltpu.make_async_copy(blk_hbm, blk, sems.at[2]),
            pltpu.make_async_copy(flat_hbm, body, sems.at[3]),
        ]
        for c in copies:
            c.start()
        meta[...] = jnp.zeros_like(meta)
        for c in copies[:3]:
            c.wait()
        w = dep[...] - base_ref[0]
        w = jnp.where(w < 0, w + wrap, w)
        k = lax.broadcasted_iota(jnp.int32, (1, slots), 1)
        for t in range(tiles):
            at = slice(t * slots, (t + 1) * slots)
            meta[0:1, at] = jnp.where(k < counts_ref[t], w[t : t + 1], DEAD).astype(jnp.float32)
            meta[1:2, at] = (blk[t, 0:1] * 8 + blk[t, 1:2]).astype(jnp.float32)
        tail[...] = meta[...].astype(jnp.bfloat16)
        last = pltpu.make_async_copy(tail, out_hbm.at[pl.ds(rows, META)], sems.at[4])
        last.start()
        copies[3].wait()
        out = pltpu.make_async_copy(body, out_hbm.at[pl.ds(0, rows)], sems.at[5])
        out.start()
        last.wait()
        out.wait()

    return pl.pallas_call(
        kernel,
        out_shape=pltpu.HBM((rows + META, size), flat.dtype),
        in_specs=[SMEM, HBM, HBM, HBM, HBM],
        out_specs=HBM,
        scratch_shapes=[
            pltpu.SMEM((tiles,), jnp.int32),
            pltpu.VMEM((tiles, slots), jnp.int32),
            pltpu.VMEM((tiles, 2, slots), jnp.int32),
            pltpu.VMEM((META, size), jnp.float32),
            pltpu.VMEM((META, size), jnp.bfloat16),
            pltpu.VMEM((rows, size), jnp.bfloat16),
            pltpu.SemaphoreType.DMA((6,)),
        ],
        compiler_params=PARAMS,
        cost_estimate=COST,
    )(base, in_hbm(counts), in_hbm(departures), in_hbm(blocks), in_hbm(flat))


def append_slots(shift, tiles, slots, where, meta_s, entries, n):
    for t in range(tiles):
        for k in range(slots):
            code = meta_s[0, t * slots + k]
            s = (code >> 6) - shift
            entries[n] = (s << 16) | ((code & 63) << 8) | (where * tiles + t)
            n = n + jnp.logical_and(s >= 0, s < tiles).astype(jnp.int32)
    return n


def add_slots(n, load, planes, size, entries, table_ref, acc_ref):
    blocks = table_ref.shape[0] // 2
    def half(i):
        entry = entries[i]
        a = load(entry & 255)
        lat_t = table_ref[(entry >> 11) & 7]
        outs = []
        for j in range(0, planes, 2):
            pair = jnp.concatenate([a[j * size : (j + 1) * size], a[(j + 1) * size : (j + 2) * size]], axis=1)
            p = jnp.dot(lat_t, pair, preferred_element_type=jnp.float32).astype(jnp.bfloat16)
            outs += [p[:, :size], p[:, size:]]
        return entry >> 16, (entry >> 8) & 7, jnp.concatenate(outs, axis=0)

    def body(i, carry):
        s0, b0, p0 = half(2 * i)
        s1, b1, p1 = half(2 * i + 1)
        q0 = jnp.dot(p0, table_ref[blocks + b0], preferred_element_type=jnp.float32)
        q1 = jnp.dot(p1, table_ref[blocks + b1], preferred_element_type=jnp.float32)
        acc_ref[s0] += q0
        acc_ref[s1] += q1
        return carry

    lax.fori_loop(0, (n + 1) >> 1, body, 0)


def ready_tables(lat, lon, later_than):
    blocks = lat.shape[0]

    def kernel(lat_hbm, lon_hbm, _, out_ref, held, sems):
        copies = [
            pltpu.make_async_copy(lat_hbm, held, sems.at[0]),
            pltpu.make_async_copy(lon_hbm, out_ref.at[pl.ds(blocks, blocks)], sems.at[1]),
        ]
        for c in copies:
            c.start()
        copies[0].wait()
        for b in range(blocks):
            out_ref[b] = held[b].T
        copies[1].wait()

    return pl.pallas_call(
        kernel,
        out_shape=jax.ShapeDtypeStruct((2 * blocks,) + lat.shape[1:], lat.dtype),
        in_specs=[HBM] * 3,
        out_specs=VMEM,
        scratch_shapes=[pltpu.VMEM(lat.shape, lat.dtype), pltpu.SemaphoreType.DMA((2,))],
        compiler_params=PARAMS,
        cost_estimate=COST,
    )(in_hbm(lat), in_hbm(lon), later_than)


def phase(sources, sign, offsets, tables, acc, coefs, tiles, slots, levels, fields, size, flops=1):
    planes = levels * fields
    rows = planes * size
    data = tiles * rows
    last = coefs is not None
    fresh = acc is None
    count = len(sources)

    def kernel(sign_ref, *refs):
        srcs, refs = refs[:count], refs[count:]
        refs = refs[1 if fresh else 2 :]
        if last:
            upper_hbm, lower_hbm, table_ref, acc_ref, up_ref, down_ref, upper_ref, lower_ref = refs[:8]
        else:
            table_ref, acc_ref = refs[:2]
        src, tail, meta_v, meta_s, entries, sems = refs[-6:]
        tails = [pltpu.make_async_copy(srcs[g].at[pl.ds(data, META)], tail.at[g], sems.at[g]) for g in range(count)]
        metas = [pltpu.make_async_copy(meta_v.at[g], meta_s.at[g], sems.at[g]) for g in range(count)]
        datas = [
            pltpu.make_async_copy(srcs[g].at[pl.ds(0, data)], src.at[pl.ds(g * data, data)], sems.at[count + g])
            for g in range(count)
        ]
        late = []
        if last:
            late = [
                pltpu.make_async_copy(upper_hbm, upper_ref, sems.at[2 * count]),
                pltpu.make_async_copy(lower_hbm, lower_ref, sems.at[2 * count + 1]),
            ]
        for c in tails + datas + late:
            c.start()
        if fresh:
            acc_ref[...] = jnp.zeros_like(acc_ref)
        for g in range(count):
            tails[g].wait()
            slot_data = tail[g].astype(jnp.float32)
            meta_v[g] = (slot_data[0:1] * 64.0 + slot_data[1:2]).astype(jnp.int32)
            metas[g].start()
        n = 0
        for g in range(count):
            metas[g].wait()
            n = append_slots((REACH - offsets[g] * sign_ref[0]) * tiles, tiles, slots, g, meta_s.at[g], entries, n)
        entries[n] = tiles << 16
        for c in datas:
            c.wait()

        def load(t):
            return src[pl.ds(pl.multiple_of(t * rows, rows), rows), :]

        add_slots(n, load, planes, size, entries, table_ref, acc_ref)
        if not last:
            return
        for c in late:
            c.wait()
        for s in range(tiles):
            u = upper_ref[s, levels - 1].astype(jnp.float32)
            d = lower_ref[s, 0].astype(jnp.float32)
            for f in range(fields):
                top = ((levels - 1) * fields + f) * size
                up_ref[s, f] = (u * acc_ref[s, top : top + size]).astype(jnp.bfloat16)
                down_ref[s, f] = (d * acc_ref[s, f * size : (f + 1) * size]).astype(jnp.bfloat16)

    args = [sign, *sources, tables]
    specs = [SMEM] + [HBM] * count + [VMEM]
    if not fresh:
        args.append(acc)
        specs.append(VMEM)
    out_shape = [jax.ShapeDtypeStruct(tables.shape, tables.dtype), jax.ShapeDtypeStruct((tiles + 1, rows, size), jnp.float32)]
    if last:
        args += [in_hbm(c) for c in coefs]
        specs += [HBM, HBM]
        out_shape += [jax.ShapeDtypeStruct((tiles, fields, size, size), jnp.bfloat16)] * 2
        out_shape += [jax.ShapeDtypeStruct(c.shape, c.dtype) for c in coefs]
    return pl.pallas_call(
        kernel,
        out_shape=out_shape,
        in_specs=specs,
        out_specs=[VMEM] * len(out_shape),
        scratch_shapes=[
            pltpu.VMEM((count * data, size), jnp.bfloat16),
            pltpu.VMEM((count, META, size), jnp.bfloat16),
            pltpu.VMEM((count, 1, size), jnp.int32),
            pltpu.SMEM((count, 1, size), jnp.int32),
            pltpu.SMEM((count * tiles * slots + 2,), jnp.int32),
            pltpu.SemaphoreType.DMA((2 * count + 2,)),
        ],
        input_output_aliases={count + 1: 0} if fresh else {count + 1: 0, count + 2: 1},
        compiler_params=PARAMS,
        cost_estimate=pl.CostEstimate(flops=flops, transcendentals=0, bytes_accessed=1),
    )(*args)


def couple(out, sums, upper, lower, rim_low, rim_up, tiles, levels, fields, size, first, last):
    own = last - first

    def kernel(sum_ref, upper_ref, lower_ref, low_ref, up_ref, *refs):
        out_ref, buf, sems = refs[-3:]
        copies = []
        for s in range(tiles):
            us = [upper_ref[s, l].astype(jnp.float32) for l in range(levels)]
            ds = [lower_ref[s, l].astype(jnp.float32) for l in range(levels)]
            for f in range(own):
                v = [sum_ref[s, (l * own + f) * size : (l * own + f + 1) * size] for l in range(levels)]
                for l in range(levels):
                    below = low_ref[s, f].astype(jnp.float32) if l == 0 else us[l - 1] * v[l - 1]
                    above = up_ref[s, f].astype(jnp.float32) if l == levels - 1 else ds[l + 1] * v[l + 1]
                    buf[s, l, f] = ((1.0 + us[l] + ds[l]) * v[l] - below - above).astype(jnp.bfloat16)
            c = pltpu.make_async_copy(buf.at[s], out_ref.at[s, :, pl.ds(first, own)], sems.at[s])
            c.start()
            copies.append(c)
        for c in copies:
            c.wait()

    args = [sums, upper, lower, rim_low, rim_up]
    specs = [VMEM] * 5
    if out is not None:
        args.append(out)
        specs.append(HBM)
    return pl.pallas_call(
        kernel,
        out_shape=jax.ShapeDtypeStruct((tiles, levels, fields, size, size), jnp.bfloat16),
        in_specs=specs,
        out_specs=HBM,
        scratch_shapes=[
            pltpu.VMEM((tiles, levels, own, size, size), jnp.bfloat16),
            pltpu.SemaphoreType.DMA((tiles,)),
        ],
        input_output_aliases={} if out is None else {5: 0},
        compiler_params=PARAMS,
        cost_estimate=COST,
    )(*args)


def passed_along(x, axis, by):
    length = lax.axis_size(axis)
    pairs = [(i, i + by) for i in range(length) if 0 <= i + by < length]
    return lax.ppermute(x, axis, pairs)


def per_device(
    adj_out, lat_weights, lon_weights, counts, departures, blocks, upper_coef, lower_coef
):
    tile_devices = lax.axis_size("tile")
    own_index = lax.axis_index("tile")
    tiles, slots = departures.shape
    levels, fields, size = adj_out.shape[1], adj_out.shape[2], adj_out.shape[3]
    planes = levels * fields
    rows = tiles * planes * size
    base_tile = ((own_index - REACH) % tile_devices * tiles).reshape(1)
    packed = pack(adj_out.reshape(rows, size), counts, departures, jnp.swapaxes(blocks, 1, 2), base_tile)

    def permuted(x, even_by, odd_by):
        pairs = [(i, (i + (even_by if i % 2 == 0 else odd_by)) % tile_devices) for i in range(tile_devices)]
        return lax.ppermute(x, "tile", pairs)

    sign = 1 - 2 * (own_index % 2)

    sign = sign.reshape(1).astype(jnp.int32)
    sizes = tiles, slots, levels, fields, size
    x_in = permuted(packed, -2, 2)
    later, tables = lax.optimization_barrier((packed, ready_tables(lat_weights, lon_weights, packed)))
    mate = permuted(later, 1, -1)
    y_in = permuted(later, 2, -2)
    tables, acc = phase((packed,), sign, (0,), tables, None, None, *sizes, O_FLOPS)
    x_in, acc = lax.optimization_barrier((x_in, acc))
    x_mate = permuted(x_in, 1, -1)
    tables, acc = phase((x_in, mate), sign, (2, 1), tables, acc, None, *sizes, M_FLOPS)
    x_mate, acc = lax.optimization_barrier((x_mate, acc))
    tables, acc = phase((x_mate,), sign, (-1,), tables, acc, None, *sizes, XM_FLOPS)
    y_in, acc = lax.optimization_barrier((y_in, acc))
    _, acc, up, down, upper, lower = phase((y_in,), sign, (-2,), tables, acc, (upper_coef, lower_coef), *sizes, L_FLOPS)
    rim_low = passed_along(up, "lev", 1)
    rim_up = passed_along(down, "lev", -1)
    return couple(None, acc, upper, lower, rim_low, rim_up, tiles, levels, fields, size, 0, fields)


def solution(mesh):
    placed = (
        P("tile", "lev", None, None, None),
        P(),
        P(),
        P("tile"),
        P("tile", None),
        P("tile", None, None),
        P("tile", "lev", None, None),
        P("tile", "lev", None, None),
    )
    return jax.shard_map(
        per_device,
        mesh=mesh,
        in_specs=placed,
        out_specs=P("tile", "lev", None, None, None),
        check_vma=False,
    )
```

time: 114 us -> 53.9 us (0.47)
  the two profiles are of different devices: /device:TPU:1 before, /device:TPU:2 now
where the time goes in v2:
time: 53.9 us; the launch traced here: 53.6 us
  starting transfers between devices  25.5 us (47%)
  waiting for transfers between devices  15.8 us (29%)
  Pallas kernels  12.3 us (23%)
    ppermute x4, starting transfers between devices, permuted(): return lax.ppermute(x, 'tile', pairs)  19.6 us
    ppermute x2, waiting for transfers between devices, passed_along(): return lax.ppermute(x, axis, pairs)  8.33 us
    pallas_call x4, Pallas kernels, phase(): pl.pallas_call(kernel, out_shape=out_shape, in_specs=specs, out_specs=[VM...  7.95 us
    ppermute x4, waiting for transfers between devices, permuted(): return lax.ppermute(x, 'tile', pairs)  7.44 us
    ppermute x2, starting transfers between devices, passed_along(): return lax.ppermute(x, axis, pairs)  5.86 us
    pallas_call x1, Pallas kernels, pack(): pl.pallas_call(kernel, out_shape=pltpu.HBM((rows + META, size), flat.dtyp...  2.1 us
    pallas_call x1, Pallas kernels, couple(): pl.pallas_call(kernel, out_shape=jax.ShapeDtypeStruct((tiles, levels, fie...  1.12 us
    pallas_call x1, Pallas kernels, ready_tables(): pl.pallas_call(kernel, out_shape=jax.ShapeDtypeStruct((2 * blocks,) + lat...  1.09 us
  transfers between devices with their start and end apart: 6, of which 5 were waited for; matrix products, arithmetic and copies ran while one was open for 0% of the time, Pallas kernels for 13%

profile of v2, /device:TPU:2, one launch (start us, length us, event | category | flops | bytes accessed | tf_op | source)
XLA Modules:
  0.0 53.6 jit_solution(3160565591990279375)
XLA Ops:
  0.0 2.1 %shard_map.82._.refs_0_ = bf16[3088,128]{1,0:T(8,128)(2,1)} custom-call(s32[1]{0:T(128)} %bitcast.1.base_ref, s32[4]{0:T(128)} %counts_hbm.1, s32[4,12]{1,0:T(4,128)} %dep_hbm.1, s32[4,2,12]{2,1,0:T(2,128)} %bitcast.5, bf16[3072,128]{1,0:T(8,128)(2,1)} %bitcast.4), custom_call_target="tpu_custom_call" | custom-call | flops 1 | bytes 1 | tf_op jit(solution)/shard_map/pallas_call | solution.py:59
  2.1 13.9 %collective-permute-start.1 = (bf16[3088,128]{1,0:T(8,128)(2,1)}, bf16[3088,128]{1,0:T(8,128)(2,1)S(1)}, u32[]{:S(2)}, u32[]{:S(2)}) collective-permute-start(bf16[3088,128]{1,0:T(8,128)(2,1)} %shard_map.82._.refs_0_), channel_id=1, source_target_pairs={{0,504},{4,12},{8,0},{12,20},{16,8},{20,28},{24,16},{28,36},{32,24... | collective-permute-start | bytes 2371592 | tf_op jit(solution)/shard_map/ppermute | solution.py:291
  16.0 1.1 %shard_map.83.refs_1_ = bf16[16,128,128]{2,1,0:T(8,128)(2,1)S(1)} custom-call(bf16[8,128,128]{2,1,0:T(8,128)(2,1)} %lat_hbm.1, bf16[8,128,128]{2,1,0:T(8,128)(2,1)} %lon_hbm.1, bf16[3088,128]{1,0:T(8,128)(2,1)} %shard_map.82._.refs_0_), custom_call_target="tpu_custom_call" | custom-call | flops 1 | bytes 1 | tf_op jit(solution)/shard_map/pallas_call | solution.py:128
  17.1 1.9 %collective-permute-start.3 = (bf16[3088,128]{1,0:T(8,128)(2,1)}, bf16[3088,128]{1,0:T(8,128)(2,1)S(1)}, u32[]{:S(2)}, u32[]{:S(2)}) collective-permute-start(bf16[3088,128]{1,0:T(8,128)(2,1)} %shard_map.82._.refs_0_), channel_id=1, source_target_pairs={{0,4},{4,0},{8,12},{12,8},{16,20},{20,16},{24,28},{28,24},{32,36},... | collective-permute-start | bytes 2371592 | tf_op jit(solution)/shard_map/ppermute | solution.py:291
  19.0 1.9 %collective-permute-start = (bf16[3088,128]{1,0:T(8,128)(2,1)}, bf16[3088,128]{1,0:T(8,128)(2,1)S(1)}, u32[]{:S(2)}, u32[]{:S(2)}) collective-permute-start(bf16[3088,128]{1,0:T(8,128)(2,1)} %shard_map.82._.refs_0_), channel_id=1, source_target_pairs={{0,8},{4,508},{8,16},{12,4},{16,24},{20,12},{24,32},{28,20},{32,40... | collective-permute-start | bytes 2371592 | tf_op jit(solution)/shard_map/ppermute | solution.py:291
  20.9 2.4 %shard_map.84 = (bf16[16,128,128]{2,1,0:T(8,128)(2,1)S(1)}, f32[5,768,128]{2,1,0:T(8,128)S(1)}) custom-call(s32[1]{0:T(128)} %bitcast.sign_ref, bf16[3088,128]{1,0:T(8,128)(2,1)} %shard_map.82._.refs_0_, bf16[16,128,128]{2,1,0:T(8,128)(2,1)S(1)} %shard_map.83.refs_1_), custom_call_target="tpu_custom_call", output_to_operand_aliasing={{0}: (2, {})} | custom-call | flops 1 | bytes 1 | tf_op jit(solution)/shard_map/pallas_call | solution.py:211
  23.3 5.1 %collective-permute-done.1.refs_0_ = bf16[3088,128]{1,0:T(8,128)(2,1)S(1)} collective-permute-done((bf16[3088,128]{1,0:T(8,128)(2,1)}, bf16[3088,128]{1,0:T(8,128)(2,1)S(1)}, u32[]{:S(2)}, u32[]{:S(2)}) %collective-permute-start.1) | collective-permute-done | bytes 790560 | tf_op jit(solution)/shard_map/ppermute | solution.py:291
  28.4 1.9 %collective-permute-start.2 = (bf16[3088,128]{1,0:T(8,128)(2,1)S(1)}, bf16[3088,128]{1,0:T(8,128)(2,1)S(1)}, u32[]{:S(2)}, u32[]{:S(2)}) collective-permute-start(bf16[3088,128]{1,0:T(8,128)(2,1)S(1)} %collective-permute-done.1.refs_0_), channel_id=1, source_target_pairs={{0,4},{4,0},{8,12},{12,8},{16,20},{20,16},{24,28},{28,24},{32,36},... | collective-permute-start | bytes 2371592 | tf_op jit(solution)/shard_map/ppermute | solution.py:291
  30.3 0.0 collective-permute-done.3.refs_1_
  30.3 2.0 %shard_map.85 = (bf16[16,128,128]{2,1,0:T(8,128)(2,1)S(1)}, f32[5,768,128]{2,1,0:T(8,128)S(1)}) custom-call(s32[1]{0:T(128)} %bitcast.sign_ref, bf16[3088,128]{1,0:T(8,128)(2,1)S(1)} %collective-permute-done.1.refs_0_, bf16[3088,128]{1,0:T(8,128)(2,1)S(1)} %collective-permute-done.3.refs_1_, ...), custom_call_target="tpu_custom_call", output_to_operand_aliasing={{0}: (3, {}), {1}: (4, {})} | custom-call | flops 68719476736 | bytes 1 | tf_op jit(solution)/shard_map/pallas_call | solution.py:211
  32.3 0.2 collective-permute-done.2.refs_0_
  32.6 1.7 %shard_map.86 = (bf16[16,128,128]{2,1,0:T(8,128)(2,1)S(1)}, f32[5,768,128]{2,1,0:T(8,128)S(1)}) custom-call(s32[1]{0:T(128)} %bitcast.sign_ref, bf16[3088,128]{1,0:T(8,128)(2,1)S(1)} %collective-permute-done.2.refs_0_, bf16[16,128,128]{2,1,0:T(8,128)(2,1)S(1)} %get-tuple-element.32.refs_1_, ...), custom_call_target="tpu_custom_call", output_to_operand_aliasing={{0}: (2, {}), {1}: (3, {})} | custom-call | flops 1 | bytes 1 | tf_op jit(solution)/shard_map/pallas_call | solution.py:211
  34.3 2.2 %collective-permute-done.refs_0_ = bf16[3088,128]{1,0:T(8,128)(2,1)S(1)} collective-permute-done((bf16[3088,128]{1,0:T(8,128)(2,1)}, bf16[3088,128]{1,0:T(8,128)(2,1)S(1)}, u32[]{:S(2)}, u32[]{:S(2)}) %collective-permute-start) | collective-permute-done | bytes 790560 | tf_op jit(solution)/shard_map/ppermute | solution.py:291
  36.5 1.8 %shard_map.87 = (bf16[16,128,128]{2,1,0:T(8,128)(2,1)S(1)}, f32[5,768,128]{2,1,0:T(8,128)S(1)}, bf16[4,3,128,128]{3,2,1,0:T(8,128)(2,1)S(1)}, bf16[4,3,128,128]{...) custom-call(s32[1]{0:T(128)} %bitcast.sign_ref, ...), custom_call_target="tpu_custom_call", output_to_operand_aliasing={{0}: (2, {}), {1}: (3, {})} | custom-call | flops 1 | bytes 1 | tf_op jit(solution)/shard_map/pallas_call | solution.py:211
  38.3 3.4 %collective-permute-start.4 = (bf16[4,3,128,128]{3,2,1,0:T(8,128)(2,1)S(1)}, bf16[4,3,128,128]{3,2,1,0:T(8,128)(2,1)S(1)}, u32[]{:S(2)}, u32[]{:S(2)}) collective-permute-start(bf16[4,3,128,128]{3,2,1,0:T(8,128)(2,1)S(1)} %get-tuple-element.41), channel_id=1, source_target_pairs={{0,1},{1,2},{2,3},{4,5},{5,6},{6,7},{8,9},{9,10},{10,11},{12,13},{... | collective-permute-start | bytes 1179656 | tf_op jit(solution)/shard_map/ppermute | solution.py:274
  41.7 2.5 %collective-permute-start.5 = (bf16[4,3,128,128]{3,2,1,0:T(8,128)(2,1)S(1)}, bf16[4,3,128,128]{3,2,1,0:T(8,128)(2,1)S(1)}, u32[]{:S(2)}, u32[]{:S(2)}) collective-permute-start(bf16[4,3,128,128]{3,2,1,0:T(8,128)(2,1)S(1)} %get-tuple-element.42), channel_id=1, source_target_pairs={{1,0},{2,1},{3,2},{5,4},{6,5},{7,6},{9,8},{10,9},{11,10},{13,12},{... | collective-permute-start | bytes 1179656 | tf_op jit(solution)/shard_map/ppermute | solution.py:274
  44.2 5.2 %collective-permute-done.4.low_ref = bf16[4,3,128,128]{3,2,1,0:T(8,128)(2,1)S(1)} collective-permute-done((bf16[4,3,128,128]{3,2,1,0:T(8,128)(2,1)S(1)}, bf16[4,3,128,128]{3,2,1,0:T(8,128)(2,1)S(1)}, u32[]{:S(2)}, u32[]{:S(2)}) %collective-permute-start.4) | collective-permute-done | bytes 393248 | tf_op jit(solution)/shard_map/ppermute | solution.py:274
  49.4 3.1 %collective-permute-done.5.up_ref = bf16[4,3,128,128]{3,2,1,0:T(8,128)(2,1)S(1)} collective-permute-done((bf16[4,3,128,128]{3,2,1,0:T(8,128)(2,1)S(1)}, bf16[4,3,128,128]{3,2,1,0:T(8,128)(2,1)S(1)}, u32[]{:S(2)}, u32[]{:S(2)}) %collective-permute-start.5) | collective-permute-done | bytes 393248 | tf_op jit(solution)/shard_map/ppermute | solution.py:274
  52.5 1.1 %shard_map.88 = bf16[4,2,3,128,128]{4,3,2,1,0:T(8,128)(2,1)} custom-call(f32[5,768,128]{2,1,0:T(8,128)S(1)} %get-tuple-element.38.sum_ref, bf16[4,2,128,128]{3,2,1,0:T(8,128)(2,1)S(1)} %get-tuple-element.39.upper_ref, bf16[4,2,128,128]{3,2,1,0:T(8,128)(2,1)S(1)} %get-tuple-element.40.lower_ref, bf16[4,3,128,128]{3,2,1,0:T(8,128)(2,1)S(1)} %collective-permute-done.4.low_ref, ...), custom_call_target="tpu_custom_call" | custom-call | flops 1 | bytes 1 | tf_op jit(solution)/shard_map/pallas_call | solution.py:256
Async XLA Ops:
  2.1 26.3 %collective-permute-start.1 = (bf16[3088,128]{1,0:T(8,128)(2,1)}, bf16[3088,128]{1,0:T(8,128)(2,1)S(1)}, u32[]{:S(2)}, u32[]{:S(2)}) collective-permute-start(bf16[3088,128]{1,0:T(8,128)(2,1)} %shard_map.82._.refs_0_), channel_id=1, source_target_pairs={{0,504},{4,12},{8,0},{12,20},{16,8},{20,28},{24,16},{28,36},{32,24... | collective-permute-start | bytes 2371592 | tf_op jit(solution)/shard_map/ppermute | solution.py:291
  17.1 13.2 %collective-permute-start.3 = (bf16[3088,128]{1,0:T(8,128)(2,1)}, bf16[3088,128]{1,0:T(8,128)(2,1)S(1)}, u32[]{:S(2)}, u32[]{:S(2)}) collective-permute-start(bf16[3088,128]{1,0:T(8,128)(2,1)} %shard_map.82._.refs_0_), channel_id=1, source_target_pairs={{0,4},{4,0},{8,12},{12,8},{16,20},{20,16},{24,28},{28,24},{32,36},... | collective-permute-start | bytes 2371592 | tf_op jit(solution)/shard_map/ppermute | solution.py:291
  19.0 17.5 %collective-permute-start = (bf16[3088,128]{1,0:T(8,128)(2,1)}, bf16[3088,128]{1,0:T(8,128)(2,1)S(1)}, u32[]{:S(2)}, u32[]{:S(2)}) collective-permute-start(bf16[3088,128]{1,0:T(8,128)(2,1)} %shard_map.82._.refs_0_), channel_id=1, source_target_pairs={{0,8},{4,508},{8,16},{12,4},{16,24},{20,12},{24,32},{28,20},{32,40... | collective-permute-start | bytes 2371592 | tf_op jit(solution)/shard_map/ppermute | solution.py:291
  28.4 4.2 %collective-permute-start.2 = (bf16[3088,128]{1,0:T(8,128)(2,1)S(1)}, bf16[3088,128]{1,0:T(8,128)(2,1)S(1)}, u32[]{:S(2)}, u32[]{:S(2)}) collective-permute-start(bf16[3088,128]{1,0:T(8,128)(2,1)S(1)} %collective-permute-done.1.refs_0_), channel_id=1, source_target_pairs={{0,4},{4,0},{8,12},{12,8},{16,20},{20,16},{24,28},{28,24},{32,36},... | collective-permute-start | bytes 2371592 | tf_op jit(solution)/shard_map/ppermute | solution.py:291
  38.3 11.1 %collective-permute-start.4 = (bf16[4,3,128,128]{3,2,1,0:T(8,128)(2,1)S(1)}, bf16[4,3,128,128]{3,2,1,0:T(8,128)(2,1)S(1)}, u32[]{:S(2)}, u32[]{:S(2)}) collective-permute-start(bf16[4,3,128,128]{3,2,1,0:T(8,128)(2,1)S(1)} %get-tuple-element.41), channel_id=1, source_target_pairs={{0,1},{1,2},{2,3},{4,5},{5,6},{6,7},{8,9},{9,10},{10,11},{12,13},{... | collective-permute-start | bytes 1179656 | tf_op jit(solution)/shard_map/ppermute | solution.py:274
  41.7 10.8 %collective-permute-start.5 = (bf16[4,3,128,128]{3,2,1,0:T(8,128)(2,1)S(1)}, bf16[4,3,128,128]{3,2,1,0:T(8,128)(2,1)S(1)}, u32[]{:S(2)}, u32[]{:S(2)}) collective-permute-start(bf16[4,3,128,128]{3,2,1,0:T(8,128)(2,1)S(1)} %get-tuple-element.42), channel_id=1, source_target_pairs={{1,0},{2,1},{3,2},{5,4},{6,5},{7,6},{9,8},{10,9},{11,10},{13,12},{... | collective-permute-start | bytes 1179656 | tf_op jit(solution)/shard_map/ppermute | solution.py:274

commit v3 on v2

v3 whole, which is shorter than its diff:
```python
import jax
import jax.numpy as jnp
from jax import lax
from jax.experimental import pallas as pl
from jax.experimental.pallas import tpu as pltpu
from jax.sharding import PartitionSpec as P

REACH = 2
DEAD = 64
META = 16
O_FLOPS = 1 << 0
M_FLOPS = 1 << 36
XM_FLOPS = 1 << 0
L_FLOPS = 1 << 0
T_FLOPS = 1 << 36
VMEM = pl.BlockSpec(memory_space=pltpu.VMEM)
SMEM = pl.BlockSpec(memory_space=pltpu.SMEM)
HBM = pl.BlockSpec(memory_space=pltpu.HBM)
COST = pl.CostEstimate(flops=1, transcendentals=0, bytes_accessed=1)
PARAMS = pltpu.CompilerParams(vmem_limit_bytes=6 << 20)


def in_hbm(x):
    return pltpu.with_memory_space_constraint(x, pltpu.HBM)


def pack(adj_out, counts, departures, blocks, base):
    tiles, levels, fields, size, _ = adj_out.shape
    rows = fields * size
    slots = departures.shape[1]
    wrap = lax.axis_size("tile") * tiles
    flat = adj_out.reshape(tiles, levels, rows, size)

    def kernel(base_ref, counts_hbm, dep_hbm, blk_hbm, flat_hbm, out_ref, counts_ref, dep, blk, meta, sems):
        copies = [
            pltpu.make_async_copy(counts_hbm, counts_ref, sems.at[0]),
            pltpu.make_async_copy(dep_hbm, dep, sems.at[1]),
            pltpu.make_async_copy(blk_hbm, blk, sems.at[2]),
        ]
        for l in range(levels):
            for t in range(tiles):
                at = (l * tiles + t) * rows + (META if l else 0)
                copies.append(
                    pltpu.make_async_copy(flat_hbm.at[t, l], out_ref.at[pl.ds(at, rows)], sems.at[3 + l * tiles + t])
                )
        for c in copies:
            c.start()
        meta[...] = jnp.zeros_like(meta)
        for c in copies[:3]:
            c.wait()
        w = dep[...] - base_ref[0]
        w = jnp.where(w < 0, w + wrap, w)
        k = lax.broadcasted_iota(jnp.int32, (1, slots), 1)
        for t in range(tiles):
            at = slice(t * slots, (t + 1) * slots)
            meta[0:1, at] = jnp.where(k < counts_ref[t], w[t : t + 1], DEAD).astype(jnp.float32)
            meta[1:2, at] = (blk[t, 0:1] * 8 + blk[t, 1:2]).astype(jnp.float32)
        out_ref[tiles * rows : tiles * rows + META, :] = meta[...].astype(jnp.bfloat16)
        for c in copies[3:]:
            c.wait()

    return pl.pallas_call(
        kernel,
        out_shape=jax.ShapeDtypeStruct((tiles * levels * rows + META, size), adj_out.dtype),
        in_specs=[SMEM, HBM, HBM, HBM, HBM],
        out_specs=VMEM,
        scratch_shapes=[
            pltpu.SMEM((tiles,), jnp.int32),
            pltpu.VMEM((tiles, slots), jnp.int32),
            pltpu.VMEM((tiles, 2, slots), jnp.int32),
            pltpu.VMEM((META, size), jnp.float32),
            pltpu.SemaphoreType.DMA((3 + tiles * levels,)),
        ],
        compiler_params=PARAMS,
        cost_estimate=COST,
    )(base, in_hbm(counts), in_hbm(departures), in_hbm(blocks), in_hbm(flat))


def append_slots(shift, tiles, slots, where, meta_s, entries, n):
    for t in range(tiles):
        for k in range(slots):
            code = meta_s[0, t * slots + k]
            s = (code >> 6) - shift
            entries[n] = (s << 16) | ((code & 63) << 8) | (where * tiles + t)
            n = n + jnp.logical_and(s >= 0, s < tiles).astype(jnp.int32)
    return n


def add_slots(n, load, planes, size, first, entries, table_ref, acc_ref):
    blocks = table_ref.shape[0] // 2
    rows = planes * size

    def half(i):
        entry = entries[i]
        a = load(entry & 255)
        lat_t = table_ref[(entry >> 11) & 7]
        outs = []
        for j in range(0, planes, 2):
            if j + 1 == planes:
                wide = a[j]
            else:
                wide = jnp.concatenate([a[j], a[j + 1]], axis=1)
            p = jnp.dot(lat_t, wide, preferred_element_type=jnp.float32).astype(jnp.bfloat16)
            outs += [p] if j + 1 == planes else [p[:, :size], p[:, size:]]
        return entry >> 16, (entry >> 8) & 7, jnp.concatenate(outs, axis=0)

    def several(start, count):
        parts = [half(start + u) for u in range(count)]
        sums = [jnp.dot(p, table_ref[blocks + b], preferred_element_type=jnp.float32) for _, b, p in parts]
        for (s, _, _), q in zip(parts, sums):
            acc_ref[s, first : first + rows, :] += q

    def four(i, carry):
        several(4 * i, 4)
        return carry

    def two(i, carry):
        several(4 * fours + 2 * i, 2)
        return carry

    fours = (n + 1) >> 2
    lax.fori_loop(0, fours, four, 0)
    lax.fori_loop(0, (jnp.maximum(n - 4 * fours, 0) + 1) >> 1, two, 0)


def ready_tables(lat, lon, later_than):
    blocks = lat.shape[0]

    def kernel(lat_hbm, lon_hbm, _, out_ref, held, sems):
        copies = [
            pltpu.make_async_copy(lat_hbm, held, sems.at[0]),
            pltpu.make_async_copy(lon_hbm, out_ref.at[pl.ds(blocks, blocks)], sems.at[1]),
        ]
        for c in copies:
            c.start()
        copies[0].wait()
        for b in range(blocks):
            out_ref[b] = held[b].T
        copies[1].wait()

    return pl.pallas_call(
        kernel,
        out_shape=jax.ShapeDtypeStruct((2 * blocks,) + lat.shape[1:], lat.dtype),
        in_specs=[HBM] * 3,
        out_specs=VMEM,
        scratch_shapes=[pltpu.VMEM(lat.shape, lat.dtype), pltpu.SemaphoreType.DMA((2,))],
        compiler_params=PARAMS,
        cost_estimate=COST,
    )(in_hbm(lat), in_hbm(lon), later_than)


def phase(sources, tails, sign, offsets, tables, acc, coefs, tiles, slots, levels, fields, size, span=None, flops=1):
    low, high = span or (0, levels)
    block = tiles * fields * size
    per_tile = fields * size
    planes = (high - low) * fields
    fresh = acc is None
    count = len(sources)
    own_tails = tails is None
    flow = coefs is not None
    held_levels = high - low

    def kernel(sign_ref, *refs):
        srcs, refs = refs[:count], refs[count:]
        if own_tails:
            tail_srcs = srcs
        else:
            tail_srcs, refs = refs[:count], refs[count:]
        refs = refs[1 if fresh else 2 :]
        if flow:
            upper_hbm, lower_hbm, table_ref, acc_ref, up_ref, down_ref, upper_ref, lower_ref = refs[:8]
        else:
            table_ref, acc_ref = refs[:2]
        src, tail, meta_v, meta_s, entries, sems = refs[-6:]
        heads = [pltpu.make_async_copy(tail_srcs[g].at[pl.ds(block, META)], tail.at[g], sems.at[g]) for g in range(count)]
        metas = [pltpu.make_async_copy(meta_v.at[g], meta_s.at[g], sems.at[g]) for g in range(count)]
        datas = []
        for g in range(count):
            for l in range(held_levels):
                at = l * block + (META if low == 0 and l > 0 else 0)
                datas.append(pltpu.make_async_copy(srcs[g].at[pl.ds(at, block)], src.at[g, l], sems.at[count + len(datas)]))
        late = []
        if flow:
            late = [
                pltpu.make_async_copy(upper_hbm, upper_ref, sems.at[count + len(datas)]),
                pltpu.make_async_copy(lower_hbm, lower_ref, sems.at[count + len(datas) + 1]),
            ]
        for c in heads + datas + late:
            c.start()
        if fresh:
            acc_ref[...] = jnp.zeros_like(acc_ref)
        for g in range(count):
            heads[g].wait()
            slot_data = tail[g].astype(jnp.float32)
            meta_v[g] = (slot_data[0:1] * 64.0 + slot_data[1:2]).astype(jnp.int32)
            metas[g].start()
        n = 0
        for g in range(count):
            metas[g].wait()
            n = append_slots((REACH - offsets[g] * sign_ref[0]) * tiles, tiles, slots, g, meta_s.at[g], entries, n)
        entries[n] = tiles << 16
        for c in datas:
            c.wait()

        def load(where):
            at = pl.ds(pl.multiple_of(where % tiles * per_tile, per_tile), per_tile)
            rows = [src[where // tiles, l, at, :] for l in range(held_levels)]
            return [r[f * size : (f + 1) * size] for r in rows for f in range(fields)]

        add_slots(n, load, planes, size, low * per_tile, entries, table_ref, acc_ref)
        if not flow:
            return
        for c in late:
            c.wait()
        top = (levels - 1) * per_tile
        for s in range(tiles):
            u = upper_ref[s, levels - 1].astype(jnp.float32)
            d = lower_ref[s, 0].astype(jnp.float32)
            for f in range(fields):
                up_ref[s, f] = (u * acc_ref[s, top + f * size : top + (f + 1) * size]).astype(jnp.bfloat16)
                down_ref[s, f] = (d * acc_ref[s, f * size : (f + 1) * size]).astype(jnp.bfloat16)

    args = [sign, *sources] + ([] if own_tails else list(tails)) + [tables]
    specs = [SMEM] + [HBM] * (len(args) - 2) + [VMEM]
    at = len(args) - 1
    if not fresh:
        args.append(acc)
        specs.append(VMEM)
    out_shape = [
        jax.ShapeDtypeStruct(tables.shape, tables.dtype),
        jax.ShapeDtypeStruct((tiles + 1, levels * per_tile, size), jnp.float32),
    ]
    if flow:
        args += [in_hbm(c) for c in coefs]
        specs += [HBM, HBM]
        out_shape += [jax.ShapeDtypeStruct((tiles, fields, size, size), jnp.bfloat16)] * 2
        out_shape += [jax.ShapeDtypeStruct(c.shape, c.dtype) for c in coefs]
    return pl.pallas_call(
        kernel,
        out_shape=out_shape,
        in_specs=specs,
        out_specs=[VMEM] * len(out_shape),
        scratch_shapes=[
            pltpu.VMEM((count, held_levels, block, size), jnp.bfloat16),
            pltpu.VMEM((count, META, size), jnp.bfloat16),
            pltpu.VMEM((count, 1, size), jnp.int32),
            pltpu.SMEM((count, 1, size), jnp.int32),
            pltpu.SMEM((count * tiles * slots + 2,), jnp.int32),
            pltpu.SemaphoreType.DMA((count * (held_levels + 1) + 2,)),
        ],
        input_output_aliases={at: 0} if fresh else {at: 0, at + 1: 1},
        compiler_params=PARAMS,
        cost_estimate=pl.CostEstimate(flops=flops, transcendentals=0, bytes_accessed=1),
    )(*args)


def couple(out, sums, upper, lower, rim, tiles, levels, fields, size, first, last, flops=1):
    own = last - first

    def kernel(sum_ref, upper_ref, lower_ref, rim_ref, *refs):
        out_ref, buf, sems = refs[-3:]
        copies = []
        for s in range(tiles):
            for l in range(first, last):
                u = upper_ref[s, l].astype(jnp.float32)
                d = lower_ref[s, l].astype(jnp.float32)
                held = 1.0 + u + d
                if l > 0:
                    from_below = upper_ref[s, l - 1].astype(jnp.float32)
                if l < levels - 1:
                    from_above = lower_ref[s, l + 1].astype(jnp.float32)
                for f in range(fields):
                    rows = [slice((m * fields + f) * size, (m * fields + f + 1) * size) for m in range(levels)]
                    edge = rim_ref[s, f].astype(jnp.float32)
                    below = edge if l == 0 else from_below * sum_ref[s, rows[l - 1], :]
                    above = edge if l == levels - 1 else from_above * sum_ref[s, rows[l + 1], :]
                    buf[s, l - first, f] = (held * sum_ref[s, rows[l], :] - below - above).astype(jnp.bfloat16)
            c = pltpu.make_async_copy(buf.at[s], out_ref.at[s, pl.ds(first, own)], sems.at[s])
            c.start()
            copies.append(c)
        for c in copies:
            c.wait()

    args = [sums, upper, lower, rim]
    specs = [VMEM] * 4
    if out is not None:
        args.append(out)
        specs.append(HBM)
    return pl.pallas_call(
        kernel,
        out_shape=jax.ShapeDtypeStruct((tiles, levels, fields, size, size), jnp.bfloat16),
        in_specs=specs,
        out_specs=HBM,
        scratch_shapes=[
            pltpu.VMEM((tiles, own, fields, size, size), jnp.bfloat16),
            pltpu.SemaphoreType.DMA((tiles,)),
        ],
        input_output_aliases={} if out is None else {4: 0},
        compiler_params=PARAMS,
        cost_estimate=pl.CostEstimate(flops=flops, transcendentals=0, bytes_accessed=1),
    )(*args)


def passed_along(x, axis, by):
    length = lax.axis_size(axis)
    pairs = [(i, i + by) for i in range(length) if 0 <= i + by < length]
    return lax.ppermute(x, axis, pairs)


def per_device(
    adj_out, lat_weights, lon_weights, counts, departures, blocks, upper_coef, lower_coef
):
    tile_devices = lax.axis_size("tile")
    own_index = lax.axis_index("tile")
    tiles, slots = departures.shape
    levels, fields, size = adj_out.shape[1], adj_out.shape[2], adj_out.shape[3]
    base_tile = ((own_index - REACH) % tile_devices * tiles).reshape(1)
    packed = pack(adj_out, counts, departures, jnp.swapaxes(blocks, 1, 2), base_tile)

    def permuted(x, even_by, odd_by):
        pairs = [(i, (i + (even_by if i % 2 == 0 else odd_by)) % tile_devices) for i in range(tile_devices)]
        return lax.ppermute(x, "tile", pairs)

    sign = 1 - 2 * (own_index % 2)

    sign = sign.reshape(1).astype(jnp.int32)
    sizes = tiles, slots, levels, fields, size
    x_in = permuted(packed, -2, 2)
    later, tables = lax.optimization_barrier((packed, ready_tables(lat_weights, lon_weights, packed)))
    mate = permuted(later, 1, -1)
    y_in = permuted(later, 2, -2)
    tables, acc = phase((packed,), None, sign, (0,), tables, None, None, *sizes, None, O_FLOPS)
    x_in, acc = lax.optimization_barrier((x_in, acc))
    x_mate = permuted(x_in, 1, -1)
    tables, acc = phase((x_in, mate), None, sign, (2, 1), tables, acc, None, *sizes, None, M_FLOPS)
    x_mate, acc = lax.optimization_barrier((x_mate, acc))
    tables, acc = phase((x_mate,), None, sign, (-1,), tables, acc, None, *sizes, None, XM_FLOPS)
    y_in, acc = lax.optimization_barrier((y_in, acc))
    coefs = upper_coef, lower_coef
    _, acc, up, down, upper, lower = phase((y_in,), None, sign, (-2,), tables, acc, coefs, *sizes, None, L_FLOPS)
    rim_low = passed_along(up, "lev", 1)
    rim_up = passed_along(down, "lev", -1)
    where = tiles, levels, fields, size
    out = couple(None, acc, upper, lower, rim_up, *where, 1, levels, T_FLOPS)
    return couple(out, acc, upper, lower, rim_low, *where, 0, 1)


def solution(mesh):
    placed = (
        P("tile", "lev", None, None, None),
        P(),
        P(),
        P("tile"),
        P("tile", None),
        P("tile", None, None),
        P("tile", "lev", None, None),
        P("tile", "lev", None, None),
    )
    return jax.shard_map(
        per_device,
        mesh=mesh,
        in_specs=placed,
        out_specs=P("tile", "lev", None, None, None),
        check_vma=False,
    )
```

time: 53.9 us -> 53.2 us (0.987)
  the two profiles are of different devices: /device:TPU:2 before, /device:TPU:6 now
where the time goes in v3:
time: 53.2 us; the launch traced here: 52.9 us
  starting transfers between devices  23.7 us (45%)
  waiting for transfers between devices  17 us (32%)
  Pallas kernels  12.1 us (23%)
    ppermute x4, starting transfers between devices, permuted(): return lax.ppermute(x, 'tile', pairs)  19.6 us
    ppermute x2, waiting for transfers between devices, passed_along(): return lax.ppermute(x, axis, pairs)  9.81 us
    pallas_call x4, Pallas kernels, phase(): pl.pallas_call(kernel, out_shape=out_shape, in_specs=specs, out_specs=[VM...  7.93 us
    ppermute x4, waiting for transfers between devices, permuted(): return lax.ppermute(x, 'tile', pairs)  7.15 us
    ppermute x2, starting transfers between devices, passed_along(): return lax.ppermute(x, axis, pairs)  4.05 us
    pallas_call x2, Pallas kernels, couple(): pl.pallas_call(kernel, out_shape=jax.ShapeDtypeStruct((tiles, levels, fie...  1.76 us
    pallas_call x1, Pallas kernels, pack(): pl.pallas_call(kernel, out_shape=jax.ShapeDtypeStruct((tiles * levels * r...  1.33 us
    pallas_call x1, Pallas kernels, ready_tables(): pl.pallas_call(kernel, out_shape=jax.ShapeDtypeStruct((2 * blocks,) + lat...  1.09 us
  transfers between devices with their start and end apart: 6, of which 4 were waited for; matrix products, arithmetic and copies ran while one was open for 0% of the time, Pallas kernels for 15%

profile of v3, /device:TPU:6, one launch (start us, length us, event | category | flops | bytes accessed | tf_op | source)
XLA Modules:
  0.0 52.9 jit_solution(4286945388765610888)
XLA Ops:
  0.0 1.3 %shard_map.82._.refs_0_ = bf16[3088,128]{1,0:T(8,128)(2,1)S(1)} custom-call(s32[1]{0:T(128)} %bitcast.1.base_ref, s32[4]{0:T(128)} %counts_hbm.1, s32[4,12]{1,0:T(4,128)} %dep_hbm.1, s32[4,2,12]{2,1,0:T(2,128)} %bitcast.5, bf16[4,2,384,128]{3,2,1,0:T(8,128)(2,1)} %bitcast.4), custom_call_target="tpu_custom_call" | custom-call | flops 1 | bytes 1 | tf_op jit(solution)/shard_map/pallas_call | solution.py:62
  1.3 13.9 %collective-permute-start.1 = (bf16[3088,128]{1,0:T(8,128)(2,1)S(1)}, bf16[3088,128]{1,0:T(8,128)(2,1)S(1)}, u32[]{:S(2)}, u32[]{:S(2)}) collective-permute-start(bf16[3088,128]{1,0:T(8,128)(2,1)S(1)} %shard_map.82._.refs_0_), channel_id=1, source_target_pairs={{0,504},{4,12},{8,0},{12,20},{16,8},{20,28},{24,16},{28,36},{32,24... | collective-permute-start | bytes 2371592 | tf_op jit(solution)/shard_map/ppermute | solution.py:322
  15.2 1.1 %shard_map.83.refs_1_ = bf16[16,128,128]{2,1,0:T(8,128)(2,1)S(1)} custom-call(bf16[8,128,128]{2,1,0:T(8,128)(2,1)} %lat_hbm.1, bf16[8,128,128]{2,1,0:T(8,128)(2,1)} %lon_hbm.1, bf16[3088,128]{1,0:T(8,128)(2,1)S(1)} %shard_map.82._.refs_0_), custom_call_target="tpu_custom_call" | custom-call | flops 1 | bytes 1 | tf_op jit(solution)/shard_map/pallas_call | solution.py:141
  16.3 1.9 %collective-permute-start.3 = (bf16[3088,128]{1,0:T(8,128)(2,1)S(1)}, bf16[3088,128]{1,0:T(8,128)(2,1)}, u32[]{:S(2)}, u32[]{:S(2)}) collective-permute-start(bf16[3088,128]{1,0:T(8,128)(2,1)S(1)} %shard_map.82._.refs_0_), channel_id=1, source_target_pairs={{0,4},{4,0},{8,12},{12,8},{16,20},{20,16},{24,28},{28,24},{32,36},... | collective-permute-start | bytes 2371592 | tf_op jit(solution)/shard_map/ppermute | solution.py:322
  18.2 1.9 %collective-permute-start = (bf16[3088,128]{1,0:T(8,128)(2,1)S(1)}, bf16[3088,128]{1,0:T(8,128)(2,1)S(1)}, u32[]{:S(2)}, u32[]{:S(2)}) collective-permute-start(bf16[3088,128]{1,0:T(8,128)(2,1)S(1)} %shard_map.82._.refs_0_), channel_id=1, source_target_pairs={{0,8},{4,508},{8,16},{12,4},{16,24},{20,12},{24,32},{28,20},{32,40... | collective-permute-start | bytes 2371592 | tf_op jit(solution)/shard_map/ppermute | solution.py:322
  20.2 1.8 %shard_map.84 = (bf16[16,128,128]{2,1,0:T(8,128)(2,1)S(1)}, f32[5,768,128]{2,1,0:T(8,128)S(1)}) custom-call(s32[1]{0:T(128)} %bitcast.sign_ref, bf16[3088,128]{1,0:T(8,128)(2,1)S(1)} %shard_map.82._.refs_0_, bf16[16,128,128]{2,1,0:T(8,128)(2,1)S(1)} %shard_map.83.refs_1_), custom_call_target="tpu_custom_call", output_to_operand_aliasing={{0}: (2, {})} | custom-call | flops 1 | bytes 1 | tf_op jit(solution)/shard_map/pallas_call | solution.py:238
  21.9 5.4 %collective-permute-done.1.refs_0_ = bf16[3088,128]{1,0:T(8,128)(2,1)S(1)} collective-permute-done((bf16[3088,128]{1,0:T(8,128)(2,1)S(1)}, bf16[3088,128]{1,0:T(8,128)(2,1)S(1)}, u32[]{:S(2)}, u32[]{:S(2)}) %collective-permute-start.1) | collective-permute-done | bytes 790560 | tf_op jit(solution)/shard_map/ppermute | solution.py:322
  27.3 1.9 %collective-permute-start.2 = (bf16[3088,128]{1,0:T(8,128)(2,1)S(1)}, bf16[3088,128]{1,0:T(8,128)(2,1)S(1)}, u32[]{:S(2)}, u32[]{:S(2)}) collective-permute-start(bf16[3088,128]{1,0:T(8,128)(2,1)S(1)} %collective-permute-done.1.refs_0_), channel_id=1, source_target_pairs={{0,4},{4,0},{8,12},{12,8},{16,20},{20,16},{24,28},{28,24},{32,36},... | collective-permute-start | bytes 2371592 | tf_op jit(solution)/shard_map/ppermute | solution.py:322
  29.2 0.0 collective-permute-done.3.refs_1_
  29.2 2.6 %shard_map.85 = (bf16[16,128,128]{2,1,0:T(8,128)(2,1)S(1)}, f32[5,768,128]{2,1,0:T(8,128)S(1)}) custom-call(s32[1]{0:T(128)} %bitcast.sign_ref, bf16[3088,128]{1,0:T(8,128)(2,1)S(1)} %collective-permute-done.1.refs_0_, bf16[3088,128]{1,0:T(8,128)(2,1)} %collective-permute-done.3.refs_1_, ...), custom_call_target="tpu_custom_call", output_to_operand_aliasing={{0}: (3, {}), {1}: (4, {})} | custom-call | flops 68719476736 | bytes 1 | tf_op jit(solution)/shard_map/pallas_call | solution.py:238
  31.9 0.0 collective-permute-done.2.refs_0_
  31.9 1.8 %shard_map.86 = (bf16[16,128,128]{2,1,0:T(8,128)(2,1)S(1)}, f32[5,768,128]{2,1,0:T(8,128)S(1)}) custom-call(s32[1]{0:T(128)} %bitcast.sign_ref, bf16[3088,128]{1,0:T(8,128)(2,1)S(1)} %collective-permute-done.2.refs_0_, bf16[16,128,128]{2,1,0:T(8,128)(2,1)S(1)} %get-tuple-element.32.refs_1_, ...), custom_call_target="tpu_custom_call", output_to_operand_aliasing={{0}: (2, {}), {1}: (3, {})} | custom-call | flops 1 | bytes 1 | tf_op jit(solution)/shard_map/pallas_call | solution.py:238
  33.7 1.8 %collective-permute-done.refs_0_ = bf16[3088,128]{1,0:T(8,128)(2,1)S(1)} collective-permute-done((bf16[3088,128]{1,0:T(8,128)(2,1)S(1)}, bf16[3088,128]{1,0:T(8,128)(2,1)S(1)}, u32[]{:S(2)}, u32[]{:S(2)}) %collective-permute-start) | collective-permute-done | bytes 790560 | tf_op jit(solution)/shard_map/ppermute | solution.py:322
  35.5 1.7 %shard_map.87 = (bf16[16,128,128]{2,1,0:T(8,128)(2,1)S(1)}, f32[5,768,128]{2,1,0:T(8,128)S(1)}, bf16[4,3,128,128]{3,2,1,0:T(8,128)(2,1)S(1)}, bf16[4,3,128,128]{...) custom-call(s32[1]{0:T(128)} %bitcast.sign_ref, ...), custom_call_target="tpu_custom_call", output_to_operand_aliasing={{0}: (2, {}), {1}: (3, {})} | custom-call | flops 1 | bytes 1 | tf_op jit(solution)/shard_map/pallas_call | solution.py:238
  37.2 2.8 %collective-permute-start.5 = (bf16[4,3,128,128]{3,2,1,0:T(8,128)(2,1)S(1)}, bf16[4,3,128,128]{3,2,1,0:T(8,128)(2,1)S(1)}, u32[]{:S(2)}, u32[]{:S(2)}) collective-permute-start(bf16[4,3,128,128]{3,2,1,0:T(8,128)(2,1)S(1)} %get-tuple-element.42), channel_id=1, source_target_pairs={{1,0},{2,1},{3,2},{5,4},{6,5},{7,6},{9,8},{10,9},{11,10},{13,12},{... | collective-permute-start | bytes 1179656 | tf_op jit(solution)/shard_map/ppermute | solution.py:307
  40.0 1.3 %collective-permute-start.4 = (bf16[4,3,128,128]{3,2,1,0:T(8,128)(2,1)S(1)}, bf16[4,3,128,128]{3,2,1,0:T(8,128)(2,1)S(1)}, u32[]{:S(2)}, u32[]{:S(2)}) collective-permute-start(bf16[4,3,128,128]{3,2,1,0:T(8,128)(2,1)S(1)} %get-tuple-element.41), channel_id=1, source_target_pairs={{0,1},{1,2},{2,3},{4,5},{5,6},{6,7},{8,9},{9,10},{10,11},{12,13},{... | collective-permute-start | bytes 1179656 | tf_op jit(solution)/shard_map/ppermute | solution.py:307
  41.3 6.6 %collective-permute-done.5.rim_ref = bf16[4,3,128,128]{3,2,1,0:T(8,128)(2,1)S(1)} collective-permute-done((bf16[4,3,128,128]{3,2,1,0:T(8,128)(2,1)S(1)}, bf16[4,3,128,128]{3,2,1,0:T(8,128)(2,1)S(1)}, u32[]{:S(2)}, u32[]{:S(2)}) %collective-permute-start.5) | collective-permute-done | bytes 393248 | tf_op jit(solution)/shard_map/ppermute | solution.py:307
  47.8 0.9 %shard_map.88.refs_0_ = bf16[4,2,3,128,128]{4,3,2,1,0:T(8,128)(2,1)} custom-call(f32[5,768,128]{2,1,0:T(8,128)S(1)} %get-tuple-element.38.sum_ref, bf16[4,2,128,128]{3,2,1,0:T(8,128)(2,1)S(1)} %get-tuple-element.39.upper_ref, bf16[4,2,128,128]{3,2,1,0:T(8,128)(2,1)S(1)} %get-tuple-element.40.lower_ref, ...), custom_call_target="tpu_custom_call" | custom-call | flops 68719476736 | bytes 1 | tf_op jit(solution)/shard_map/pallas_call | solution.py:289
  48.7 3.2 %collective-permute-done.4.rim_ref = bf16[4,3,128,128]{3,2,1,0:T(8,128)(2,1)S(1)} collective-permute-done((bf16[4,3,128,128]{3,2,1,0:T(8,128)(2,1)S(1)}, bf16[4,3,128,128]{3,2,1,0:T(8,128)(2,1)S(1)}, u32[]{:S(2)}, u32[]{:S(2)}) %collective-permute-start.4) | collective-permute-done | bytes 393248 | tf_op jit(solution)/shard_map/ppermute | solution.py:307
  52.0 0.9 %shard_map.89 = bf16[4,2,3,128,128]{4,3,2,1,0:T(8,128)(2,1)} custom-call(f32[5,768,128]{2,1,0:T(8,128)S(1)} %get-tuple-element.38.sum_ref, bf16[4,2,128,128]{3,2,1,0:T(8,128)(2,1)S(1)} %get-tuple-element.39.upper_ref, bf16[4,2,128,128]{3,2,1,0:T(8,128)(2,1)S(1)} %get-tuple-element.40.lower_ref, ...), custom_call_target="tpu_custom_call", output_to_operand_aliasing={{}: (4, {})} | custom-call | flops 1 | bytes 1 | tf_op jit(solution)/shard_map/pallas_call | solution.py:289
Async XLA Ops:
  1.3 26.0 %collective-permute-start.1 = (bf16[3088,128]{1,0:T(8,128)(2,1)S(1)}, bf16[3088,128]{1,0:T(8,128)(2,1)S(1)}, u32[]{:S(2)}, u32[]{:S(2)}) collective-permute-start(bf16[3088,128]{1,0:T(8,128)(2,1)S(1)} %shard_map.82._.refs_0_), channel_id=1, source_target_pairs={{0,504},{4,12},{8,0},{12,20},{16,8},{20,28},{24,16},{28,36},{32,24... | collective-permute-start | bytes 2371592 | tf_op jit(solution)/shard_map/ppermute | solution.py:322
  16.3 12.9 %collective-permute-start.3 = (bf16[3088,128]{1,0:T(8,128)(2,1)S(1)}, bf16[3088,128]{1,0:T(8,128)(2,1)}, u32[]{:S(2)}, u32[]{:S(2)}) collective-permute-start(bf16[3088,128]{1,0:T(8,128)(2,1)S(1)} %shard_map.82._.refs_0_), channel_id=1, source_target_pairs={{0,4},{4,0},{8,12},{12,8},{16,20},{20,16},{24,28},{28,24},{32,36},... | collective-permute-start | bytes 2371592 | tf_op jit(solution)/shard_map/ppermute | solution.py:322
  18.2 17.2 %collective-permute-start = (bf16[3088,128]{1,0:T(8,128)(2,1)S(1)}, bf16[3088,128]{1,0:T(8,128)(2,1)S(1)}, u32[]{:S(2)}, u32[]{:S(2)}) collective-permute-start(bf16[3088,128]{1,0:T(8,128)(2,1)S(1)} %shard_map.82._.refs_0_), channel_id=1, source_target_pairs={{0,8},{4,508},{8,16},{12,4},{16,24},{20,12},{24,32},{28,20},{32,40... | collective-permute-start | bytes 2371592 | tf_op jit(solution)/shard_map/ppermute | solution.py:322
  27.3 4.6 %collective-permute-start.2 = (bf16[3088,128]{1,0:T(8,128)(2,1)S(1)}, bf16[3088,128]{1,0:T(8,128)(2,1)S(1)}, u32[]{:S(2)}, u32[]{:S(2)}) collective-permute-start(bf16[3088,128]{1,0:T(8,128)(2,1)S(1)} %collective-permute-done.1.refs_0_), channel_id=1, source_target_pairs={{0,4},{4,0},{8,12},{12,8},{16,20},{20,16},{24,28},{28,24},{32,36},... | collective-permute-start | bytes 2371592 | tf_op jit(solution)/shard_map/ppermute | solution.py:322
  37.2 10.6 %collective-permute-start.5 = (bf16[4,3,128,128]{3,2,1,0:T(8,128)(2,1)S(1)}, bf16[4,3,128,128]{3,2,1,0:T(8,128)(2,1)S(1)}, u32[]{:S(2)}, u32[]{:S(2)}) collective-permute-start(bf16[4,3,128,128]{3,2,1,0:T(8,128)(2,1)S(1)} %get-tuple-element.42), channel_id=1, source_target_pairs={{1,0},{2,1},{3,2},{5,4},{6,5},{7,6},{9,8},{10,9},{11,10},{13,12},{... | collective-permute-start | bytes 1179656 | tf_op jit(solution)/shard_map/ppermute | solution.py:307
  40.0 12.0 %collective-permute-start.4 = (bf16[4,3,128,128]{3,2,1,0:T(8,128)(2,1)S(1)}, bf16[4,3,128,128]{3,2,1,0:T(8,128)(2,1)S(1)}, u32[]{:S(2)}, u32[]{:S(2)}) collective-permute-start(bf16[4,3,128,128]{3,2,1,0:T(8,128)(2,1)S(1)} %get-tuple-element.41), channel_id=1, source_target_pairs={{0,1},{1,2},{2,3},{4,5},{5,6},{6,7},{8,9},{9,10},{10,11},{12,13},{... | collective-permute-start | bytes 1179656 | tf_op jit(solution)/shard_map/ppermute | solution.py:307

commit v4 on v3

--- a/solution.py
+++ b/solution.py
@@ -149,65 +149,50 @@
     )(in_hbm(lat), in_hbm(lon), later_than)
 
 
-def phase(sources, tails, sign, offsets, tables, acc, coefs, tiles, slots, levels, fields, size, span=None, flops=1):
-    low, high = span or (0, levels)
+def phase(sources, sign, offsets, tables, acc, coefs, tiles, slots, levels, fields, size, flops=1):
     block = tiles * fields * size
     per_tile = fields * size
-    planes = (high - low) * fields
+    planes = levels * fields
     fresh = acc is None
     count = len(sources)
-    own_tails = tails is None
     flow = coefs is not None
-    held_levels = high - low
 
     def kernel(sign_ref, *refs):
         srcs, refs = refs[:count], refs[count:]
-        if own_tails:
-            tail_srcs = srcs
-        else:
-            tail_srcs, refs = refs[:count], refs[count:]
         refs = refs[1 if fresh else 2 :]
         if flow:
             upper_hbm, lower_hbm, table_ref, acc_ref, up_ref, down_ref, upper_ref, lower_ref = refs[:8]
         else:
             table_ref, acc_ref = refs[:2]
-        src, tail, meta_v, meta_s, entries, sems = refs[-6:]
-        heads = [pltpu.make_async_copy(tail_srcs[g].at[pl.ds(block, META)], tail.at[g], sems.at[g]) for g in range(count)]
+        meta_v, meta_s, entries, sems = refs[-4:]
         metas = [pltpu.make_async_copy(meta_v.at[g], meta_s.at[g], sems.at[g]) for g in range(count)]
-        datas = []
-        for g in range(count):
-            for l in range(held_levels):
-                at = l * block + (META if low == 0 and l > 0 else 0)
-                datas.append(pltpu.make_async_copy(srcs[g].at[pl.ds(at, block)], src.at[g, l], sems.at[count + len(datas)]))
         late = []
         if flow:
             late = [
-                pltpu.make_async_copy(upper_hbm, upper_ref, sems.at[count + len(datas)]),
-                pltpu.make_async_copy(lower_hbm, lower_ref, sems.at[count + len(datas) + 1]),
+                pltpu.make_async_copy(upper_hbm, upper_ref, sems.at[count]),
+                pltpu.make_async_copy(lower_hbm, lower_ref, sems.at[count + 1]),
             ]
-        for c in heads + datas + late:
+        for c in late:
             c.start()
+        for g in range(count):
+            slot_data = srcs[g][block : block + META, :].astype(jnp.float32)
+            meta_v[g] = (slot_data[0:1] * 64.0 + slot_data[1:2]).astype(jnp.int32)
+            metas[g].start()
         if fresh:
             acc_ref[...] = jnp.zeros_like(acc_ref)
         for g in range(count):
-            heads[g].wait()
-            slot_data = tail[g].astype(jnp.float32)
-            meta_v[g] = (slot_data[0:1] * 64.0 + slot_data[1:2]).astype(jnp.int32)
-            metas[g].start()
-        n = 0
-        for g in range(count):
             metas[g].wait()
-            n = append_slots((REACH - offsets[g] * sign_ref[0]) * tiles, tiles, slots, g, meta_s.at[g], entries, n)
-        entries[n] = tiles << 16
-        for c in datas:
-            c.wait()
-
-        def load(where):
-            at = pl.ds(pl.multiple_of(where % tiles * per_tile, per_tile), per_tile)
-            rows = [src[where // tiles, l, at, :] for l in range(held_levels)]
-            return [r[f * size : (f + 1) * size] for r in rows for f in range(fields)]
-
-        add_slots(n, load, planes, size, low * per_tile, entries, table_ref, acc_ref)
+            n = append_slots((REACH - offsets[g] * sign_ref[0]) * tiles, tiles, slots, 0, meta_s.at[g], entries, 0)
+            entries[n] = tiles << 16
+
+            def load(t, ref=srcs[g]):
+                rows = []
+                for l in range(levels):
+                    at = pl.multiple_of(t * per_tile, per_tile) + (l * block + META if l else 0)
+                    rows.append(ref[pl.ds(pl.multiple_of(at, 16), per_tile), :])
+                return [r[f * size : (f + 1) * size] for r in rows for f in range(fields)]
+
+            add_slots(n, load, planes, size, 0, entries, table_ref, acc_ref)
         if not flow:
             return
         for c in late:
@@ -220,8 +205,8 @@
                 up_ref[s, f] = (u * acc_ref[s, top + f * size : top + (f + 1) * size]).astype(jnp.bfloat16)
                 down_ref[s, f] = (d * acc_ref[s, f * size : (f + 1) * size]).astype(jnp.bfloat16)
 
-    args = [sign, *sources] + ([] if own_tails else list(tails)) + [tables]
-    specs = [SMEM] + [HBM] * (len(args) - 2) + [VMEM]
+    args = [sign, *sources, tables]
+    specs = [SMEM] + [VMEM] * (count + 1)
     at = len(args) - 1
     if not fresh:
         args.append(acc)
@@ -241,12 +226,10 @@
         in_specs=specs,
         out_specs=[VMEM] * len(out_shape),
         scratch_shapes=[
-            pltpu.VMEM((count, held_levels, block, size), jnp.bfloat16),
-            pltpu.VMEM((count, META, size), jnp.bfloat16),
             pltpu.VMEM((count, 1, size), jnp.int32),
             pltpu.SMEM((count, 1, size), jnp.int32),
-            pltpu.SMEM((count * tiles * slots + 2,), jnp.int32),
-            pltpu.SemaphoreType.DMA((count * (held_levels + 1) + 2,)),
+            pltpu.SMEM((tiles * slots + 2,), jnp.int32),
+            pltpu.SemaphoreType.DMA((count + 2,)),
         ],
         input_output_aliases={at: 0} if fresh else {at: 0, at + 1: 1},
         compiler_params=PARAMS,
@@ -326,18 +309,19 @@
     sign = sign.reshape(1).astype(jnp.int32)
     sizes = tiles, slots, levels, fields, size
     x_in = permuted(packed, -2, 2)
-    later, tables = lax.optimization_barrier((packed, ready_tables(lat_weights, lon_weights, packed)))
-    mate = permuted(later, 1, -1)
-    y_in = permuted(later, 2, -2)
-    tables, acc = phase((packed,), None, sign, (0,), tables, None, None, *sizes, None, O_FLOPS)
+    mate, tables = lax.optimization_barrier((packed, ready_tables(lat_weights, lon_weights, packed)))
+    mate = permuted(mate, 1, -1)
+    tables, acc = phase((packed,), sign, (0,), tables, None, None, *sizes, O_FLOPS)
+    y_in, acc = lax.optimization_barrier((packed, acc))
+    y_in = permuted(y_in, 2, -2)
     x_in, acc = lax.optimization_barrier((x_in, acc))
     x_mate = permuted(x_in, 1, -1)
-    tables, acc = phase((x_in, mate), None, sign, (2, 1), tables, acc, None, *sizes, None, M_FLOPS)
+    tables, acc = phase((x_in, mate), sign, (2, 1), tables, acc, None, *sizes, M_FLOPS)
     x_mate, acc = lax.optimization_barrier((x_mate, acc))
-    tables, acc = phase((x_mate,), None, sign, (-1,), tables, acc, None, *sizes, None, XM_FLOPS)
+    tables, acc = phase((x_mate,), sign, (-1,), tables, acc, None, *sizes, XM_FLOPS)
     y_in, acc = lax.optimization_barrier((y_in, acc))
     coefs = upper_coef, lower_coef
-    _, acc, up, down, upper, lower = phase((y_in,), None, sign, (-2,), tables, acc, coefs, *sizes, None, L_FLOPS)
+    _, acc, up, down, upper, lower = phase((y_in,), sign, (-2,), tables, acc, coefs, *sizes, L_FLOPS)
     rim_low = passed_along(up, "lev", 1)
     rim_up = passed_along(down, "lev", -1)
     where = tiles, levels, fields, size

time: 53.2 us -> 52.6 us (0.989)
    ppermute x2, waiting for transfers between devices: 9.81 us -> 7.48 us  [passed_along(): return lax.ppermute(x, axis, pairs)]
    ppermute x4, waiting for transfers between devices: 7.15 us -> 9.26 us  [permuted(): return lax.ppermute(x, 'tile', pairs)]
  transfers between devices with their start and end apart: 6 -> 6, of which waited for: 4 -> 5; matrix products, arithmetic and copies ran while one was open for 0% -> 0% of each run, Pallas kernels for 15% -> 15%
where the time goes in v4:
time: 52.6 us; the launch traced here: 52.3 us
  starting transfers between devices  23.7 us (45%)
  waiting for transfers between devices  16.7 us (32%)
  Pallas kernels  11.8 us (22%)
    ppermute x4, starting transfers between devices, permuted(): return lax.ppermute(x, 'tile', pairs)  19.6 us
    ppermute x4, waiting for transfers between devices, permuted(): return lax.ppermute(x, 'tile', pairs)  9.26 us
    pallas_call x4, Pallas kernels, phase(): pl.pallas_call(kernel, out_shape=out_shape, in_specs=specs, out_specs=[VM...  7.59 us
    ppermute x2, waiting for transfers between devices, passed_along(): return lax.ppermute(x, axis, pairs)  7.48 us
    ppermute x2, starting transfers between devices, passed_along(): return lax.ppermute(x, axis, pairs)  4.05 us
    pallas_call x2, Pallas kernels, couple(): pl.pallas_call(kernel, out_shape=jax.ShapeDtypeStruct((tiles, levels, fie...  1.76 us
    pallas_call x1, Pallas kernels, pack(): pl.pallas_call(kernel, out_shape=jax.ShapeDtypeStruct((tiles * levels * r...  1.33 us
    pallas_call x1, Pallas kernels, ready_tables(): pl.pallas_call(kernel, out_shape=jax.ShapeDtypeStruct((2 * blocks,) + lat...  1.09 us
  transfers between devices with their start and end apart: 6, of which 5 were waited for; matrix products, arithmetic and copies ran while one was open for 0% of the time, Pallas kernels for 15%

profile of v4, /device:TPU:6, one launch (start us, length us, event | category | flops | bytes accessed | tf_op | source)
XLA Modules:
  0.0 52.3 jit_solution(4699878772030399783)
XLA Ops:
  0.0 1.3 %shard_map.82._.refs_0_ = bf16[3088,128]{1,0:T(8,128)(2,1)S(1)} custom-call(s32[1]{0:T(128)} %bitcast.1.base_ref, s32[4]{0:T(128)} %counts_hbm.1, s32[4,12]{1,0:T(4,128)} %dep_hbm.1, s32[4,2,12]{2,1,0:T(2,128)} %bitcast.5, bf16[4,2,384,128]{3,2,1,0:T(8,128)(2,1)} %bitcast.4), custom_call_target="tpu_custom_call" | custom-call | flops 1 | bytes 1 | tf_op jit(solution)/shard_map/pallas_call | solution.py:62
  1.3 13.9 %collective-permute-start.1 = (bf16[3088,128]{1,0:T(8,128)(2,1)S(1)}, bf16[3088,128]{1,0:T(8,128)(2,1)S(1)}, u32[]{:S(2)}, u32[]{:S(2)}) collective-permute-start(bf16[3088,128]{1,0:T(8,128)(2,1)S(1)} %shard_map.82._.refs_0_), channel_id=1, source_target_pairs={{0,504},{4,12},{8,0},{12,20},{16,8},{20,28},{24,16},{28,36},{32,24... | collective-permute-start | bytes 2371592 | tf_op jit(solution)/shard_map/ppermute | solution.py:305
  15.2 1.1 %shard_map.83.refs_1_ = bf16[16,128,128]{2,1,0:T(8,128)(2,1)S(1)} custom-call(bf16[8,128,128]{2,1,0:T(8,128)(2,1)} %lat_hbm.1, bf16[8,128,128]{2,1,0:T(8,128)(2,1)} %lon_hbm.1, bf16[3088,128]{1,0:T(8,128)(2,1)S(1)} %shard_map.82._.refs_0_), custom_call_target="tpu_custom_call" | custom-call | flops 1 | bytes 1 | tf_op jit(solution)/shard_map/pallas_call | solution.py:141
  16.3 1.9 %collective-permute-start.3 = (bf16[3088,128]{1,0:T(8,128)(2,1)S(1)}, bf16[3088,128]{1,0:T(8,128)(2,1)S(1)}, u32[]{:S(2)}, u32[]{:S(2)}) collective-permute-start(bf16[3088,128]{1,0:T(8,128)(2,1)S(1)} %shard_map.82._.refs_0_), channel_id=1, source_target_pairs={{0,4},{4,0},{8,12},{12,8},{16,20},{20,16},{24,28},{28,24},{32,36},... | collective-permute-start | bytes 2371592 | tf_op jit(solution)/shard_map/ppermute | solution.py:305
  18.2 1.5 %shard_map.84 = (bf16[16,128,128]{2,1,0:T(8,128)(2,1)S(1)}, f32[5,768,128]{2,1,0:T(8,128)S(1)}) custom-call(s32[1]{0:T(128)} %bitcast.sign_ref, bf16[3088,128]{1,0:T(8,128)(2,1)S(1)} %shard_map.82._.refs_0_, bf16[16,128,128]{2,1,0:T(8,128)(2,1)S(1)} %shard_map.83.refs_1_), custom_call_target="tpu_custom_call", output_to_operand_aliasing={{0}: (2, {})} | custom-call | flops 1 | bytes 1 | tf_op jit(solution)/shard_map/pallas_call | solution.py:223
  19.8 1.9 %collective-permute-start = (bf16[3088,128]{1,0:T(8,128)(2,1)S(1)}, bf16[3088,128]{1,0:T(8,128)(2,1)S(1)}, u32[]{:S(2)}, u32[]{:S(2)}) collective-permute-start(bf16[3088,128]{1,0:T(8,128)(2,1)S(1)} %shard_map.82._.refs_0_), channel_id=1, source_target_pairs={{0,8},{4,508},{8,16},{12,4},{16,24},{20,12},{24,32},{28,20},{32,40... | collective-permute-start | bytes 2371592 | tf_op jit(solution)/shard_map/ppermute | solution.py:305
  21.7 3.6 %collective-permute-done.1.refs_0_ = bf16[3088,128]{1,0:T(8,128)(2,1)S(1)} collective-permute-done((bf16[3088,128]{1,0:T(8,128)(2,1)S(1)}, bf16[3088,128]{1,0:T(8,128)(2,1)S(1)}, u32[]{:S(2)}, u32[]{:S(2)}) %collective-permute-start.1) | collective-permute-done | bytes 790560 | tf_op jit(solution)/shard_map/ppermute | solution.py:305
  25.3 1.9 %collective-permute-start.2 = (bf16[3088,128]{1,0:T(8,128)(2,1)S(1)}, bf16[3088,128]{1,0:T(8,128)(2,1)S(1)}, u32[]{:S(2)}, u32[]{:S(2)}) collective-permute-start(bf16[3088,128]{1,0:T(8,128)(2,1)S(1)} %collective-permute-done.1.refs_0_), channel_id=1, source_target_pairs={{0,4},{4,0},{8,12},{12,8},{16,20},{20,16},{24,28},{28,24},{32,36},... | collective-permute-start | bytes 2371592 | tf_op jit(solution)/shard_map/ppermute | solution.py:305
  27.2 0.0 collective-permute-done.3.refs_1_
  27.3 2.1 %shard_map.85 = (bf16[16,128,128]{2,1,0:T(8,128)(2,1)S(1)}, f32[5,768,128]{2,1,0:T(8,128)S(1)}) custom-call(s32[1]{0:T(128)} %bitcast.sign_ref, bf16[3088,128]{1,0:T(8,128)(2,1)S(1)} %collective-permute-done.1.refs_0_, bf16[3088,128]{1,0:T(8,128)(2,1)S(1)} %collective-permute-done.3.refs_1_, ...), custom_call_target="tpu_custom_call", output_to_operand_aliasing={{0}: (3, {}), {1}: (4, {})} | custom-call | flops 68719476736 | bytes 1 | tf_op jit(solution)/shard_map/pallas_call | solution.py:223
  29.4 0.2 collective-permute-done.2.refs_0_
  29.5 2.0 %shard_map.86 = (bf16[16,128,128]{2,1,0:T(8,128)(2,1)S(1)}, f32[5,768,128]{2,1,0:T(8,128)S(1)}) custom-call(s32[1]{0:T(128)} %bitcast.sign_ref, bf16[3088,128]{1,0:T(8,128)(2,1)S(1)} %collective-permute-done.2.refs_0_, bf16[16,128,128]{2,1,0:T(8,128)(2,1)S(1)} %get-tuple-element.36.refs_1_, ...), custom_call_target="tpu_custom_call", output_to_operand_aliasing={{0}: (2, {}), {1}: (3, {})} | custom-call | flops 1 | bytes 1 | tf_op jit(solution)/shard_map/pallas_call | solution.py:223
  31.5 5.5 %collective-permute-done.refs_0_ = bf16[3088,128]{1,0:T(8,128)(2,1)S(1)} collective-permute-done((bf16[3088,128]{1,0:T(8,128)(2,1)S(1)}, bf16[3088,128]{1,0:T(8,128)(2,1)S(1)}, u32[]{:S(2)}, u32[]{:S(2)}) %collective-permute-start) | collective-permute-done | bytes 790560 | tf_op jit(solution)/shard_map/ppermute | solution.py:305
  37.0 1.9 %shard_map.87 = (bf16[16,128,128]{2,1,0:T(8,128)(2,1)S(1)}, f32[5,768,128]{2,1,0:T(8,128)S(1)}, bf16[4,3,128,128]{3,2,1,0:T(8,128)(2,1)S(1)}, bf16[4,3,128,128]{...) custom-call(s32[1]{0:T(128)} %bitcast.sign_ref, ...), custom_call_target="tpu_custom_call", output_to_operand_aliasing={{0}: (2, {}), {1}: (3, {})} | custom-call | flops 1 | bytes 1 | tf_op jit(solution)/shard_map/pallas_call | solution.py:223
  39.0 2.8 %collective-permute-start.5 = (bf16[4,3,128,128]{3,2,1,0:T(8,128)(2,1)S(1)}, bf16[4,3,128,128]{3,2,1,0:T(8,128)(2,1)S(1)}, u32[]{:S(2)}, u32[]{:S(2)}) collective-permute-start(bf16[4,3,128,128]{3,2,1,0:T(8,128)(2,1)S(1)} %get-tuple-element.46), channel_id=1, source_target_pairs={{1,0},{2,1},{3,2},{5,4},{6,5},{7,6},{9,8},{10,9},{11,10},{13,12},{... | collective-permute-start | bytes 1179656 | tf_op jit(solution)/shard_map/ppermute | solution.py:290
  41.7 1.3 %collective-permute-start.4 = (bf16[4,3,128,128]{3,2,1,0:T(8,128)(2,1)S(1)}, bf16[4,3,128,128]{3,2,1,0:T(8,128)(2,1)S(1)}, u32[]{:S(2)}, u32[]{:S(2)}) collective-permute-start(bf16[4,3,128,128]{3,2,1,0:T(8,128)(2,1)S(1)} %get-tuple-element.45), channel_id=1, source_target_pairs={{0,1},{1,2},{2,3},{4,5},{5,6},{6,7},{8,9},{9,10},{10,11},{12,13},{... | collective-permute-start | bytes 1179656 | tf_op jit(solution)/shard_map/ppermute | solution.py:290
  43.0 4.0 %collective-permute-done.5.rim_ref = bf16[4,3,128,128]{3,2,1,0:T(8,128)(2,1)S(1)} collective-permute-done((bf16[4,3,128,128]{3,2,1,0:T(8,128)(2,1)S(1)}, bf16[4,3,128,128]{3,2,1,0:T(8,128)(2,1)S(1)}, u32[]{:S(2)}, u32[]{:S(2)}) %collective-permute-start.5) | collective-permute-done | bytes 393248 | tf_op jit(solution)/shard_map/ppermute | solution.py:290
  47.0 0.9 %shard_map.88.refs_0_ = bf16[4,2,3,128,128]{4,3,2,1,0:T(8,128)(2,1)} custom-call(f32[5,768,128]{2,1,0:T(8,128)S(1)} %get-tuple-element.42.sum_ref, bf16[4,2,128,128]{3,2,1,0:T(8,128)(2,1)S(1)} %get-tuple-element.43.upper_ref, bf16[4,2,128,128]{3,2,1,0:T(8,128)(2,1)S(1)} %get-tuple-element.44.lower_ref, ...), custom_call_target="tpu_custom_call" | custom-call | flops 68719476736 | bytes 1 | tf_op jit(solution)/shard_map/pallas_call | solution.py:272
  47.9 3.5 %collective-permute-done.4.rim_ref = bf16[4,3,128,128]{3,2,1,0:T(8,128)(2,1)S(1)} collective-permute-done((bf16[4,3,128,128]{3,2,1,0:T(8,128)(2,1)S(1)}, bf16[4,3,128,128]{3,2,1,0:T(8,128)(2,1)S(1)}, u32[]{:S(2)}, u32[]{:S(2)}) %collective-permute-start.4) | collective-permute-done | bytes 393248 | tf_op jit(solution)/shard_map/ppermute | solution.py:290
  51.4 0.9 %shard_map.89 = bf16[4,2,3,128,128]{4,3,2,1,0:T(8,128)(2,1)} custom-call(f32[5,768,128]{2,1,0:T(8,128)S(1)} %get-tuple-element.42.sum_ref, bf16[4,2,128,128]{3,2,1,0:T(8,128)(2,1)S(1)} %get-tuple-element.43.upper_ref, bf16[4,2,128,128]{3,2,1,0:T(8,128)(2,1)S(1)} %get-tuple-element.44.lower_ref, ...), custom_call_target="tpu_custom_call", output_to_operand_aliasing={{}: (4, {})} | custom-call | flops 1 | bytes 1 | tf_op jit(solution)/shard_map/pallas_call | solution.py:272
Async XLA Ops:
  1.3 24.0 %collective-permute-start.1 = (bf16[3088,128]{1,0:T(8,128)(2,1)S(1)}, bf16[3088,128]{1,0:T(8,128)(2,1)S(1)}, u32[]{:S(2)}, u32[]{:S(2)}) collective-permute-start(bf16[3088,128]{1,0:T(8,128)(2,1)S(1)} %shard_map.82._.refs_0_), channel_id=1, source_target_pairs={{0,504},{4,12},{8,0},{12,20},{16,8},{20,28},{24,16},{28,36},{32,24... | collective-permute-start | bytes 2371592 | tf_op jit(solution)/shard_map/ppermute | solution.py:305
  16.3 10.9 %collective-permute-start.3 = (bf16[3088,128]{1,0:T(8,128)(2,1)S(1)}, bf16[3088,128]{1,0:T(8,128)(2,1)S(1)}, u32[]{:S(2)}, u32[]{:S(2)}) collective-permute-start(bf16[3088,128]{1,0:T(8,128)(2,1)S(1)} %shard_map.82._.refs_0_), channel_id=1, source_target_pairs={{0,4},{4,0},{8,12},{12,8},{16,20},{20,16},{24,28},{28,24},{32,36},... | collective-permute-start | bytes 2371592 | tf_op jit(solution)/shard_map/ppermute | solution.py:305
  19.8 17.2 %collective-permute-start = (bf16[3088,128]{1,0:T(8,128)(2,1)S(1)}, bf16[3088,128]{1,0:T(8,128)(2,1)S(1)}, u32[]{:S(2)}, u32[]{:S(2)}) collective-permute-start(bf16[3088,128]{1,0:T(8,128)(2,1)S(1)} %shard_map.82._.refs_0_), channel_id=1, source_target_pairs={{0,8},{4,508},{8,16},{12,4},{16,24},{20,12},{24,32},{28,20},{32,40... | collective-permute-start | bytes 2371592 | tf_op jit(solution)/shard_map/ppermute | solution.py:305
  25.3 4.2 %collective-permute-start.2 = (bf16[3088,128]{1,0:T(8,128)(2,1)S(1)}, bf16[3088,128]{1,0:T(8,128)(2,1)S(1)}, u32[]{:S(2)}, u32[]{:S(2)}) collective-permute-start(bf16[3088,128]{1,0:T(8,128)(2,1)S(1)} %collective-permute-done.1.refs_0_), channel_id=1, source_target_pairs={{0,4},{4,0},{8,12},{12,8},{16,20},{20,16},{24,28},{28,24},{32,36},... | collective-permute-start | bytes 2371592 | tf_op jit(solution)/shard_map/ppermute | solution.py:305
  39.0 8.0 %collective-permute-start.5 = (bf16[4,3,128,128]{3,2,1,0:T(8,128)(2,1)S(1)}, bf16[4,3,128,128]{3,2,1,0:T(8,128)(2,1)S(1)}, u32[]{:S(2)}, u32[]{:S(2)}) collective-permute-start(bf16[4,3,128,128]{3,2,1,0:T(8,128)(2,1)S(1)} %get-tuple-element.46), channel_id=1, source_target_pairs={{1,0},{2,1},{3,2},{5,4},{6,5},{7,6},{9,8},{10,9},{11,10},{13,12},{... | collective-permute-start | bytes 1179656 | tf_op jit(solution)/shard_map/ppermute | solution.py:290
  41.7 9.7 %collective-permute-start.4 = (bf16[4,3,128,128]{3,2,1,0:T(8,128)(2,1)S(1)}, bf16[4,3,128,128]{3,2,1,0:T(8,128)(2,1)S(1)}, u32[]{:S(2)}, u32[]{:S(2)}) collective-permute-start(bf16[4,3,128,128]{3,2,1,0:T(8,128)(2,1)S(1)} %get-tuple-element.45), channel_id=1, source_target_pairs={{0,1},{1,2},{2,3},{4,5},{5,6},{6,7},{8,9},{9,10},{10,11},{12,13},{... | collective-permute-start | bytes 1179656 | tf_op jit(solution)/shard_map/ppermute | solution.py:290

commit v5 on v4

--- a/solution.py
+++ b/solution.py
@@ -123,32 +123,6 @@
     lax.fori_loop(0, (jnp.maximum(n - 4 * fours, 0) + 1) >> 1, two, 0)
 
 
-def ready_tables(lat, lon, later_than):
-    blocks = lat.shape[0]
-
-    def kernel(lat_hbm, lon_hbm, _, out_ref, held, sems):
-        copies = [
-            pltpu.make_async_copy(lat_hbm, held, sems.at[0]),
-            pltpu.make_async_copy(lon_hbm, out_ref.at[pl.ds(blocks, blocks)], sems.at[1]),
-        ]
-        for c in copies:
-            c.start()
-        copies[0].wait()
-        for b in range(blocks):
-            out_ref[b] = held[b].T
-        copies[1].wait()
-
-    return pl.pallas_call(
-        kernel,
-        out_shape=jax.ShapeDtypeStruct((2 * blocks,) + lat.shape[1:], lat.dtype),
-        in_specs=[HBM] * 3,
-        out_specs=VMEM,
-        scratch_shapes=[pltpu.VMEM(lat.shape, lat.dtype), pltpu.SemaphoreType.DMA((2,))],
-        compiler_params=PARAMS,
-        cost_estimate=COST,
-    )(in_hbm(lat), in_hbm(lon), later_than)
-
-
 def phase(sources, sign, offsets, tables, acc, coefs, tiles, slots, levels, fields, size, flops=1):
     block = tiles * fields * size
     per_tile = fields * size
@@ -159,18 +133,25 @@
 
     def kernel(sign_ref, *refs):
         srcs, refs = refs[:count], refs[count:]
-        refs = refs[1 if fresh else 2 :]
+        lat_hbm, lon_hbm = refs[:2]
+        refs = refs[2:]
         if flow:
             upper_hbm, lower_hbm, table_ref, acc_ref, up_ref, down_ref, upper_ref, lower_ref = refs[:8]
         else:
             table_ref, acc_ref = refs[:2]
-        meta_v, meta_s, entries, sems = refs[-4:]
+        meta_v, meta_s, entries, sems = refs[-5:-1] if fresh else refs[-4:]
+        held = refs[-1]
         metas = [pltpu.make_async_copy(meta_v.at[g], meta_s.at[g], sems.at[g]) for g in range(count)]
         late = []
         if flow:
             late = [
                 pltpu.make_async_copy(upper_hbm, upper_ref, sems.at[count]),
                 pltpu.make_async_copy(lower_hbm, lower_ref, sems.at[count + 1]),
+            ]
+        if fresh:
+            late = [
+                pltpu.make_async_copy(lat_hbm, held, sems.at[count]),
+                pltpu.make_async_copy(lon_hbm, table_ref.at[pl.ds(lon_hbm.shape[0], lon_hbm.shape[0])], sems.at[count + 1]),
             ]
         for c in late:
             c.start()
@@ -184,6 +165,11 @@
             metas[g].wait()
             n = append_slots((REACH - offsets[g] * sign_ref[0]) * tiles, tiles, slots, 0, meta_s.at[g], entries, 0)
             entries[n] = tiles << 16
+            if fresh and g == 0:
+                for c in late:
+                    c.wait()
+                for b in range(lat_hbm.shape[0]):
+                    table_ref[b] = held[b].T
 
             def load(t, ref=srcs[g]):
                 rows = []
@@ -205,14 +191,20 @@
                 up_ref[s, f] = (u * acc_ref[s, top + f * size : top + (f + 1) * size]).astype(jnp.bfloat16)
                 down_ref[s, f] = (d * acc_ref[s, f * size : (f + 1) * size]).astype(jnp.bfloat16)
 
-    args = [sign, *sources, tables]
-    specs = [SMEM] + [VMEM] * (count + 1)
+    if fresh:
+        args = [sign, *sources] + [in_hbm(t) for t in tables]
+        specs = [SMEM] + [VMEM] * count + [HBM] * 2
+        table_shape = (tables[0].shape[0] + tables[1].shape[0],) + tables[0].shape[1:]
+    else:
+        args = [sign, *sources, tables]
+        specs = [SMEM] + [VMEM] * (count + 1)
+        table_shape = tables.shape
     at = len(args) - 1
     if not fresh:
         args.append(acc)
         specs.append(VMEM)
     out_shape = [
-        jax.ShapeDtypeStruct(tables.shape, tables.dtype),
+        jax.ShapeDtypeStruct(table_shape, sources[0].dtype),
         jax.ShapeDtypeStruct((tiles + 1, levels * per_tile, size), jnp.float32),
     ]
     if flow:
@@ -230,8 +222,9 @@
             pltpu.SMEM((count, 1, size), jnp.int32),
             pltpu.SMEM((tiles * slots + 2,), jnp.int32),
             pltpu.SemaphoreType.DMA((count + 2,)),
-        ],
-        input_output_aliases={at: 0} if fresh else {at: 0, at + 1: 1},
+        ]
+        + ([pltpu.VMEM(tables[0].shape, tables[0].dtype)] if fresh else []),
+        input_output_aliases={} if fresh else {at: 0, at + 1: 1},
         compiler_params=PARAMS,
         cost_estimate=pl.CostEstimate(flops=flops, transcendentals=0, bytes_accessed=1),
     )(*args)
@@ -309,11 +302,10 @@
     sign = sign.reshape(1).astype(jnp.int32)
     sizes = tiles, slots, levels, fields, size
     x_in = permuted(packed, -2, 2)
-    mate, tables = lax.optimization_barrier((packed, ready_tables(lat_weights, lon_weights, packed)))
-    mate = permuted(mate, 1, -1)
-    tables, acc = phase((packed,), sign, (0,), tables, None, None, *sizes, O_FLOPS)
-    y_in, acc = lax.optimization_barrier((packed, acc))
-    y_in = permuted(y_in, 2, -2)
+    tables, acc = phase((packed,), sign, (0,), (lat_weights, lon_weights), None, None, *sizes, O_FLOPS)
+    later, acc = lax.optimization_barrier((packed, acc))
+    mate = permuted(later, 1, -1)
+    y_in = permuted(later, 2, -2)
     x_in, acc = lax.optimization_barrier((x_in, acc))
     x_mate = permuted(x_in, 1, -1)
     tables, acc = phase((x_in, mate), sign, (2, 1), tables, acc, None, *sizes, M_FLOPS)

time: 52.6 us -> 52 us (0.989)
  Pallas kernels: 11.8 us -> 10.4 us
  waiting for transfers between devices: 16.7 us -> 17.7 us
    pallas_call x1 -> x0, Pallas kernels: 1.09 us -> none  [ready_tables(): pl.pallas_call(kernel, out_shape=jax.ShapeDtypeStruct((2 * blocks,) + lat...]
    ppermute x4, waiting for transfers between devices: 9.26 us -> 10.2 us  [permuted(): return lax.ppermute(x, 'tile', pairs)]
  transfers between devices with their start and end apart: 6 -> 6, of which waited for: 5 -> 5; matrix products, arithmetic and copies ran while one was open for 0% -> 0% of each run, Pallas kernels for 15% -> 12%
where the time goes in v5:
time: 52 us; the launch traced here: 51.9 us
  starting transfers between devices  23.7 us (46%)
  waiting for transfers between devices  17.7 us (34%)
  Pallas kernels  10.4 us (20%)
    ppermute x4, starting transfers between devices, permuted(): return lax.ppermute(x, 'tile', pairs)  19.6 us
    ppermute x4, waiting for transfers between devices, permuted(): return lax.ppermute(x, 'tile', pairs)  10.2 us
    ppermute x2, waiting for transfers between devices, passed_along(): return lax.ppermute(x, axis, pairs)  7.48 us
    pallas_call x4, Pallas kernels, phase(): pl.pallas_call(kernel, out_shape=out_shape, in_specs=specs, out_specs=[VM...  7.32 us
    ppermute x2, starting transfers between devices, passed_along(): return lax.ppermute(x, axis, pairs)  4.05 us
    pallas_call x2, Pallas kernels, couple(): pl.pallas_call(kernel, out_shape=jax.ShapeDtypeStruct((tiles, levels, fie...  1.76 us
    pallas_call x1, Pallas kernels, pack(): pl.pallas_call(kernel, out_shape=jax.ShapeDtypeStruct((tiles * levels * r...  1.33 us
  transfers between devices with their start and end apart: 6, of which 5 were waited for; matrix products, arithmetic and copies ran while one was open for 0% of the time, Pallas kernels for 12%

profile of v5, /device:TPU:6, one launch (start us, length us, event | category | flops | bytes accessed | tf_op | source)
XLA Modules:
  0.0 51.9 jit_solution(1050253701268339107)
XLA Ops:
  0.0 1.3 %shard_map.82.refs_0_ = bf16[3088,128]{1,0:T(8,128)(2,1)S(1)} custom-call(s32[1]{0:T(128)} %bitcast.1.base_ref, s32[4]{0:T(128)} %counts_hbm.1, s32[4,12]{1,0:T(4,128)} %dep_hbm.1, s32[4,2,12]{2,1,0:T(2,128)} %bitcast.5, bf16[4,2,384,128]{3,2,1,0:T(8,128)(2,1)} %bitcast.4), custom_call_target="tpu_custom_call" | custom-call | flops 1 | bytes 1 | tf_op jit(solution)/shard_map/pallas_call | solution.py:62
  1.3 13.9 %collective-permute-start.1 = (bf16[3088,128]{1,0:T(8,128)(2,1)S(1)}, bf16[3088,128]{1,0:T(8,128)(2,1)S(1)}, u32[]{:S(2)}, u32[]{:S(2)}) collective-permute-start(bf16[3088,128]{1,0:T(8,128)(2,1)S(1)} %shard_map.82.refs_0_), channel_id=1, source_target_pairs={{0,504},{4,12},{8,0},{12,20},{16,8},{20,28},{24,16},{28,36},{32,24... | collective-permute-start | bytes 2371592 | tf_op jit(solution)/shard_map/ppermute | solution.py:298
  15.2 2.2 %shard_map.83 = (bf16[16,128,128]{2,1,0:T(8,128)(2,1)S(1)}, f32[5,768,128]{2,1,0:T(8,128)S(1)}) custom-call(s32[1]{0:T(128)} %bitcast.sign_ref, bf16[3088,128]{1,0:T(8,128)(2,1)S(1)} %shard_map.82.refs_0_, bf16[8,128,128]{2,1,0:T(8,128)(2,1)} %refs_1_.1, bf16[8,128,128]{2,1,0:T(8,128)(2,1)} %refs_2_.1), custom_call_target="tpu_custom_call" | custom-call | flops 1 | bytes 1 | tf_op jit(solution)/shard_map/pallas_call | solution.py:215
  17.5 1.9 %collective-permute-start.3 = (bf16[3088,128]{1,0:T(8,128)(2,1)S(1)}, bf16[3088,128]{1,0:T(8,128)(2,1)S(1)}, u32[]{:S(2)}, u32[]{:S(2)}) collective-permute-start(bf16[3088,128]{1,0:T(8,128)(2,1)S(1)} %shard_map.82.refs_0_), channel_id=1, source_target_pairs={{0,4},{4,0},{8,12},{12,8},{16,20},{20,16},{24,28},{28,24},{32,36},... | collective-permute-start | bytes 2371592 | tf_op jit(solution)/shard_map/ppermute | solution.py:298
  19.4 1.9 %collective-permute-start = (bf16[3088,128]{1,0:T(8,128)(2,1)S(1)}, bf16[3088,128]{1,0:T(8,128)(2,1)S(1)}, u32[]{:S(2)}, u32[]{:S(2)}) collective-permute-start(bf16[3088,128]{1,0:T(8,128)(2,1)S(1)} %shard_map.82.refs_0_), channel_id=1, source_target_pairs={{0,8},{4,508},{8,16},{12,4},{16,24},{20,12},{24,32},{28,20},{32,40... | collective-permute-start | bytes 2371592 | tf_op jit(solution)/shard_map/ppermute | solution.py:298
  21.3 5.3 %collective-permute-done.1.refs_0_ = bf16[3088,128]{1,0:T(8,128)(2,1)S(1)} collective-permute-done((bf16[3088,128]{1,0:T(8,128)(2,1)S(1)}, bf16[3088,128]{1,0:T(8,128)(2,1)S(1)}, u32[]{:S(2)}, u32[]{:S(2)}) %collective-permute-start.1) | collective-permute-done | bytes 790560 | tf_op jit(solution)/shard_map/ppermute | solution.py:298
  26.6 1.9 %collective-permute-start.2 = (bf16[3088,128]{1,0:T(8,128)(2,1)S(1)}, bf16[3088,128]{1,0:T(8,128)(2,1)S(1)}, u32[]{:S(2)}, u32[]{:S(2)}) collective-permute-start(bf16[3088,128]{1,0:T(8,128)(2,1)S(1)} %collective-permute-done.1.refs_0_), channel_id=1, source_target_pairs={{0,4},{4,0},{8,12},{12,8},{16,20},{20,16},{24,28},{28,24},{32,36},... | collective-permute-start | bytes 2371592 | tf_op jit(solution)/shard_map/ppermute | solution.py:298
  28.5 0.0 collective-permute-done.3.refs_1_
  28.5 1.9 %shard_map.84 = (bf16[16,128,128]{2,1,0:T(8,128)(2,1)S(1)}, f32[5,768,128]{2,1,0:T(8,128)S(1)}) custom-call(s32[1]{0:T(128)} %bitcast.sign_ref, bf16[3088,128]{1,0:T(8,128)(2,1)S(1)} %collective-permute-done.1.refs_0_, bf16[3088,128]{1,0:T(8,128)(2,1)S(1)} %collective-permute-done.3.refs_1_, ...), custom_call_target="tpu_custom_call", output_to_operand_aliasing={{0}: (3, {}), {1}: (4, {})} | custom-call | flops 68719476736 | bytes 1 | tf_op jit(solution)/shard_map/pallas_call | solution.py:215
  30.4 0.3 collective-permute-done.2.refs_0_
  30.8 1.2 %shard_map.85 = (bf16[16,128,128]{2,1,0:T(8,128)(2,1)S(1)}, f32[5,768,128]{2,1,0:T(8,128)S(1)}) custom-call(s32[1]{0:T(128)} %bitcast.sign_ref, bf16[3088,128]{1,0:T(8,128)(2,1)S(1)} %collective-permute-done.2.refs_0_, bf16[16,128,128]{2,1,0:T(8,128)(2,1)S(1)} %get-tuple-element.32.refs_1_, ...), custom_call_target="tpu_custom_call", output_to_operand_aliasing={{0}: (2, {}), {1}: (3, {})} | custom-call | flops 1 | bytes 1 | tf_op jit(solution)/shard_map/pallas_call | solution.py:215
  32.0 4.6 %collective-permute-done.refs_0_ = bf16[3088,128]{1,0:T(8,128)(2,1)S(1)} collective-permute-done((bf16[3088,128]{1,0:T(8,128)(2,1)S(1)}, bf16[3088,128]{1,0:T(8,128)(2,1)S(1)}, u32[]{:S(2)}, u32[]{:S(2)}) %collective-permute-start) | collective-permute-done | bytes 790560 | tf_op jit(solution)/shard_map/ppermute | solution.py:298
  36.6 1.9 %shard_map.86 = (bf16[16,128,128]{2,1,0:T(8,128)(2,1)S(1)}, f32[5,768,128]{2,1,0:T(8,128)S(1)}, bf16[4,3,128,128]{3,2,1,0:T(8,128)(2,1)S(1)}, bf16[4,3,128,128]{...) custom-call(s32[1]{0:T(128)} %bitcast.sign_ref, ...), custom_call_target="tpu_custom_call", output_to_operand_aliasing={{0}: (2, {}), {1}: (3, {})} | custom-call | flops 1 | bytes 1 | tf_op jit(solution)/shard_map/pallas_call | solution.py:215
  38.6 2.8 %collective-permute-start.5 = (bf16[4,3,128,128]{3,2,1,0:T(8,128)(2,1)S(1)}, bf16[4,3,128,128]{3,2,1,0:T(8,128)(2,1)S(1)}, u32[]{:S(2)}, u32[]{:S(2)}) collective-permute-start(bf16[4,3,128,128]{3,2,1,0:T(8,128)(2,1)S(1)} %get-tuple-element.42), channel_id=1, source_target_pairs={{1,0},{2,1},{3,2},{5,4},{6,5},{7,6},{9,8},{10,9},{11,10},{13,12},{... | collective-permute-start | bytes 1179656 | tf_op jit(solution)/shard_map/ppermute | solution.py:283
  41.4 1.3 %collective-permute-start.4 = (bf16[4,3,128,128]{3,2,1,0:T(8,128)(2,1)S(1)}, bf16[4,3,128,128]{3,2,1,0:T(8,128)(2,1)S(1)}, u32[]{:S(2)}, u32[]{:S(2)}) collective-permute-start(bf16[4,3,128,128]{3,2,1,0:T(8,128)(2,1)S(1)} %get-tuple-element.41), channel_id=1, source_target_pairs={{0,1},{1,2},{2,3},{4,5},{5,6},{6,7},{8,9},{9,10},{10,11},{12,13},{... | collective-permute-start | bytes 1179656 | tf_op jit(solution)/shard_map/ppermute | solution.py:283
  42.7 4.0 %collective-permute-done.5.rim_ref = bf16[4,3,128,128]{3,2,1,0:T(8,128)(2,1)S(1)} collective-permute-done((bf16[4,3,128,128]{3,2,1,0:T(8,128)(2,1)S(1)}, bf16[4,3,128,128]{3,2,1,0:T(8,128)(2,1)S(1)}, u32[]{:S(2)}, u32[]{:S(2)}) %collective-permute-start.5) | collective-permute-done | bytes 393248 | tf_op jit(solution)/shard_map/ppermute | solution.py:283
  46.6 0.9 %shard_map.87.refs_0_ = bf16[4,2,3,128,128]{4,3,2,1,0:T(8,128)(2,1)} custom-call(f32[5,768,128]{2,1,0:T(8,128)S(1)} %get-tuple-element.38.sum_ref, bf16[4,2,128,128]{3,2,1,0:T(8,128)(2,1)S(1)} %get-tuple-element.39.upper_ref, bf16[4,2,128,128]{3,2,1,0:T(8,128)(2,1)S(1)} %get-tuple-element.40.lower_ref, ...), custom_call_target="tpu_custom_call" | custom-call | flops 68719476736 | bytes 1 | tf_op jit(solution)/shard_map/pallas_call | solution.py:265
  47.5 3.5 %collective-permute-done.4.rim_ref = bf16[4,3,128,128]{3,2,1,0:T(8,128)(2,1)S(1)} collective-permute-done((bf16[4,3,128,128]{3,2,1,0:T(8,128)(2,1)S(1)}, bf16[4,3,128,128]{3,2,1,0:T(8,128)(2,1)S(1)}, u32[]{:S(2)}, u32[]{:S(2)}) %collective-permute-start.4) | collective-permute-done | bytes 393248 | tf_op jit(solution)/shard_map/ppermute | solution.py:283
  51.0 0.9 %shard_map.88 = bf16[4,2,3,128,128]{4,3,2,1,0:T(8,128)(2,1)} custom-call(f32[5,768,128]{2,1,0:T(8,128)S(1)} %get-tuple-element.38.sum_ref, bf16[4,2,128,128]{3,2,1,0:T(8,128)(2,1)S(1)} %get-tuple-element.39.upper_ref, bf16[4,2,128,128]{3,2,1,0:T(8,128)(2,1)S(1)} %get-tuple-element.40.lower_ref, ...), custom_call_target="tpu_custom_call", output_to_operand_aliasing={{}: (4, {})} | custom-call | flops 1 | bytes 1 | tf_op jit(solution)/shard_map/pallas_call | solution.py:265
Async XLA Ops:
  1.3 25.2 %collective-permute-start.1 = (bf16[3088,128]{1,0:T(8,128)(2,1)S(1)}, bf16[3088,128]{1,0:T(8,128)(2,1)S(1)}, u32[]{:S(2)}, u32[]{:S(2)}) collective-permute-start(bf16[3088,128]{1,0:T(8,128)(2,1)S(1)} %shard_map.82.refs_0_), channel_id=1, source_target_pairs={{0,504},{4,12},{8,0},{12,20},{16,8},{20,28},{24,16},{28,36},{32,24... | collective-permute-start | bytes 2371592 | tf_op jit(solution)/shard_map/ppermute | solution.py:298
  17.5 11.0 %collective-permute-start.3 = (bf16[3088,128]{1,0:T(8,128)(2,1)S(1)}, bf16[3088,128]{1,0:T(8,128)(2,1)S(1)}, u32[]{:S(2)}, u32[]{:S(2)}) collective-permute-start(bf16[3088,128]{1,0:T(8,128)(2,1)S(1)} %shard_map.82.refs_0_), channel_id=1, source_target_pairs={{0,4},{4,0},{8,12},{12,8},{16,20},{20,16},{24,28},{28,24},{32,36},... | collective-permute-start | bytes 2371592 | tf_op jit(solution)/shard_map/ppermute | solution.py:298
  19.4 17.2 %collective-permute-start = (bf16[3088,128]{1,0:T(8,128)(2,1)S(1)}, bf16[3088,128]{1,0:T(8,128)(2,1)S(1)}, u32[]{:S(2)}, u32[]{:S(2)}) collective-permute-start(bf16[3088,128]{1,0:T(8,128)(2,1)S(1)} %shard_map.82.refs_0_), channel_id=1, source_target_pairs={{0,8},{4,508},{8,16},{12,4},{16,24},{20,12},{24,32},{28,20},{32,40... | collective-permute-start | bytes 2371592 | tf_op jit(solution)/shard_map/ppermute | solution.py:298
  26.6 4.2 %collective-permute-start.2 = (bf16[3088,128]{1,0:T(8,128)(2,1)S(1)}, bf16[3088,128]{1,0:T(8,128)(2,1)S(1)}, u32[]{:S(2)}, u32[]{:S(2)}) collective-permute-start(bf16[3088,128]{1,0:T(8,128)(2,1)S(1)} %collective-permute-done.1.refs_0_), channel_id=1, source_target_pairs={{0,4},{4,0},{8,12},{12,8},{16,20},{20,16},{24,28},{28,24},{32,36},... | collective-permute-start | bytes 2371592 | tf_op jit(solution)/shard_map/ppermute | solution.py:298
  38.6 8.0 %collective-permute-start.5 = (bf16[4,3,128,128]{3,2,1,0:T(8,128)(2,1)S(1)}, bf16[4,3,128,128]{3,2,1,0:T(8,128)(2,1)S(1)}, u32[]{:S(2)}, u32[]{:S(2)}) collective-permute-start(bf16[4,3,128,128]{3,2,1,0:T(8,128)(2,1)S(1)} %get-tuple-element.42), channel_id=1, source_target_pairs={{1,0},{2,1},{3,2},{5,4},{6,5},{7,6},{9,8},{10,9},{11,10},{13,12},{... | collective-permute-start | bytes 1179656 | tf_op jit(solution)/shard_map/ppermute | solution.py:283
  41.4 9.7 %collective-permute-start.4 = (bf16[4,3,128,128]{3,2,1,0:T(8,128)(2,1)S(1)}, bf16[4,3,128,128]{3,2,1,0:T(8,128)(2,1)S(1)}, u32[]{:S(2)}, u32[]{:S(2)}) collective-permute-start(bf16[4,3,128,128]{3,2,1,0:T(8,128)(2,1)S(1)} %get-tuple-element.41), channel_id=1, source_target_pairs={{0,1},{1,2},{2,3},{4,5},{5,6},{6,7},{8,9},{9,10},{10,11},{12,13},{... | collective-permute-start | bytes 1179656 | tf_op jit(solution)/shard_map/ppermute | solution.py:283
